TPU v7x, 32 devices: a whole 2x2x4 slice. The times are simulated.
32 devices in a mesh: grp: 2 (over y), atoms: 4 (over z), feat: 2 (over x), rep: 2 (over core).
Axes of the slice: x: 2, y: 2, z: 4, core: 2. Of those that a mesh axis runs over, the one named last changes fastest.
Arguments:
- atom_coords: bfloat16 [4, 2048, 3, 3072], P(('grp', 'rep'), None, None, 'atoms'), parts along dimension 0, may hold values from -9 to 9
- atom_pairs: int32 [2, 1024], P(None, 'feat'), may hold values from 0 to 3071, as said below
- traj_ids: int32 [4, 2048], P(('grp', 'rep')), parts along dimension 0, may hold values from 0 to 7, never falling along the last dimension, each value on 1 to 512 neighbouring positions
Outputs:
- corr_inst: float32 [2048, 1024], P(('grp', 'atoms', 'rep'), 'feat'), parts along dimension 0
- corr_lag: float32 [2048, 1024], P(('grp', 'atoms', 'rep'), 'feat'), parts along dimension 0
- projections: float32 [4, 2048, 1024], P(('grp', 'rep'), 'atoms', 'feat'), parts along dimension 0
There are 2 independent parts, one for each index of `grp`. A program takes and returns all parts, laid end to end along the dimension named above; an argument that names none is the same for every part. Nothing has to cross between parts.
Inputs may be any that keep to these rules, and one draw needn't show every extreme that they name: `atom_pairs`: the two atoms of a feature differ. `traj_ids`: trajectory numbers never fall along a replica stream; some trajectory holds exactly 512 frames.
All inputs are finite; a program needn't handle non-finite values.
Results may differ from a plain program's by a relative error of at most 0.0003.
Values may be sent and summed in bfloat16 or wider, within the bound.
A program may use at most 128 MiB of HBM per device.

v0:
```python
import jax
import jax.numpy as jnp
from jax import lax
from jax.sharding import PartitionSpec as P

LAG = 10


def passed_along(block, axis, distance):
    devices = range(lax.axis_size(axis))
    route = [(i - distance, i) for i in devices if i - distance in devices]
    return lax.ppermute(block, axis, route)


def featurize(positions, pairs):
    first = jnp.take(positions, pairs[0], axis=2)
    second = jnp.take(positions, pairs[1], axis=2)
    delta = first - second
    return jnp.sqrt(jnp.sum(delta * delta, axis=1) + 0.01)


def cross_moment(left, right):
    return lax.dot_general(
        left,
        right,
        (((0,), (0,)), ((), ())),
        precision=lax.Precision.HIGHEST,
        preferred_element_type=jnp.float32,
    )


def shards(atom_coords, atom_pairs, traj_ids):
    atom_groups = lax.axis_size("atoms")
    feat_groups = lax.axis_size("feat")
    frames_here = atom_coords.shape[1] // atom_groups
    width_atoms = atom_coords.shape[3]
    atom_index = lax.axis_index("atoms")
    feat_index = lax.axis_index("feat")
    col_width = atom_pairs.shape[1]
    used_pairs = lax.all_gather(atom_pairs, "feat", axis=1, tiled=True)
    quarter = frames_here // feat_groups
    grouped = atom_coords.reshape(1, atom_groups, feat_groups, quarter, 3, width_atoms)
    blocks = lax.dynamic_slice_in_dim(grouped, feat_index, 1, 2).reshape(
        1, atom_groups, quarter, 3, width_atoms
    )
    computed = featurize(
        lax.all_to_all(blocks, "atoms", split_axis=1, concat_axis=4, tiled=True)[0, 0].astype(
            jnp.float32
        ),
        used_pairs,
    )
    every = lax.all_gather(computed, "feat", axis=0, tiled=True)
    own = lax.dynamic_slice_in_dim(every, feat_index * col_width, col_width, 1)
    incoming = passed_along(own[:LAG], "atoms", -1)
    future = jnp.concatenate([own[LAG:], incoming], 0)
    ids = jnp.concatenate([traj_ids[0], jnp.full((LAG,), -1, jnp.int32)])
    offset = atom_index * frames_here
    ids_now = lax.dynamic_slice_in_dim(ids, offset, frames_here)
    ids_later = lax.dynamic_slice_in_dim(ids, offset + LAG, frames_here)
    valid = (ids_now == ids_later).astype(jnp.float32)[:, None]
    count, total_now, total_next = lax.psum(
        (jnp.sum(valid), jnp.sum(valid * every, 0), jnp.sum(valid * future, 0)), ("atoms", "rep")
    )
    mean_now = total_now / count
    mean_next = total_next / count
    centered = every - mean_now
    own_centered = lax.dynamic_slice_in_dim(centered, feat_index * col_width, col_width, 1)
    future_centered = future - mean_next
    right_side = jnp.concatenate([valid * own_centered, valid * future_centered], 1)
    spread_now_part = jnp.sum(valid * centered * centered, 0)
    spread_next_part = jnp.sum(valid * future_centered * future_centered, 0)
    row_count = every.shape[1] // lax.axis_size(("atoms", "rep"))
    row_start = lax.axis_index(("atoms", "rep")) * row_count
    local_moments = cross_moment(centered, right_side)
    summed, spread_now, spread_next = lax.psum(
        (local_moments, spread_now_part, spread_next_part), ("atoms", "rep")
    )
    mine = lax.dynamic_slice_in_dim(summed, row_start, row_count, 0)
    scale_now = 1.0 / jnp.sqrt(spread_now / count + 1e-05)
    scale_next = 1.0 / jnp.sqrt(spread_next / count + 1e-05)
    scale_rows = lax.dynamic_slice_in_dim(scale_now, row_start, row_count)
    scale_cols = lax.dynamic_slice_in_dim(scale_now, feat_index * col_width, col_width)
    corr_inst = mine[:, :col_width] / count * scale_rows[:, None] * scale_cols[None, :]
    corr_lag = mine[:, col_width:] / count * scale_rows[:, None] * scale_next[None, :]
    projections = (own_centered * scale_cols)[None]
    return (corr_inst, corr_lag, projections)


def solution(mesh):
    placed = (P(("grp", "rep"), None, None, "atoms"), P(None, "feat"), P(("grp", "rep"), None))
    return jax.shard_map(
        shards,
        mesh=mesh,
        in_specs=placed,
        out_specs=(
            P(("grp", "atoms", "rep"), "feat"),
            P(("grp", "atoms", "rep"), "feat"),
            P(("grp", "rep"), "atoms", "feat"),
        ),
        check_vma=False,
    )
```

profile of v0, /device:TPU:0, one launch (start us, length us, event | category | flops | bytes accessed | tf_op | source)
XLA Modules:
  0.0 383.3 jit_solution(13211677239903812215)
XLA Ops:
  7.2 4.8 %constant_dynamic-slice_fusion.1 = bf16[1,4,1,256,3,768]{5,3,2,1,4,0:T(8,128)(2,1)} fusion(bf16[1,4,2,256,3,768]{5,3,2,1,4,0:T(8,128)(2,1)} %bitcast.24, s32[]{:T(128)S(6)} %select_n.25), kind=kLoop, calls=%fused_computation.42 | loop fusion | bytes 9437188 | tf_op jit(solution)/shard_map/dynamic_slice | solution.py:43
  12.0 6.6 %copy.14 = bf16[1,4,1,256,3,768]{3,5,4,1,2,0:T(8,128)(2,1)} copy(bf16[1,4,1,256,3,768]{5,3,2,1,4,0:T(8,128)(2,1)} %constant_dynamic-slice_fusion.1) | data formatting | bytes 9437184
  18.6 6.5 %all-to-all-start = ((bf16[1,4,256,3,768]{2,4,3,0,1:T(8,128)(2,1)}), bf16[1,4,256,3,768]{2,4,3,0,1:T(8,128)(2,1)}, u32[]{:S(2)}, u32[]{:S(2)}) async-start(bf16[1,4,256,3,768]{2,4,3,0,1:T(8,128)(2,1)} %bitcast.23), calls=%async_computation | async-start | bytes 9437184 | tf_op jit(solution)/shard_map/all_to_all | solution.py:47
  25.1 4.4 %all_gather.6 = s32[2,1024]{1,0:T(2,128)S(1)} all-gather(s32[2,512]{1,0:T(2,128)S(1)} %copy-done.2), channel_id=1, replica_groups=mesh['grp'=2,'atoms'=4,'feat'=2,'rep'=2] {'feat'}, dimensions={1}, use_global_device_ids=true | all-gather | bytes 12288 | tf_op jit(solution)/shard_map/all_gather | solution.py:40
  29.5 100.3 %all-to-all-done = bf16[1,4,256,3,768]{2,4,3,0,1:T(8,128)(2,1)} async-done(((bf16[1,4,256,3,768]{2,4,3,0,1:T(8,128)(2,1)}), bf16[1,4,256,3,768]{2,4,3,0,1:T(8,128)(2,1)}, u32[]{:S(2)}, u32[]{:S(2)}) %all-to-all-start) | async-done | bytes 4718624 | tf_op jit(solution)/shard_map/all_to_all | solution.py:47
  129.8 3.3 bitcast_convert_fusion
  133.1 22.2 %copy.11 = f32[256,3,3072]{0,1,2:T(4,128)} copy(f32[256,3,3072]{0,2,1:T(8,128)S(1)} %bitcast.22) | data formatting | bytes 18874368 | tf_op jit(solution)/shard_map/convert_element_type | solution.py:47
  155.3 14.2 %gather_fusion = f32[1024,256,3]{1,2,0:T(4,128)} fusion(f32[256,3,3072]{0,1,2:T(4,128)} %copy.11, s32[1024]{0:T(1024)S(1)} %fusion.11), kind=kCustom, calls=%fused_computation.clone | custom fusion | bytes 6295552 | tf_op jit(solution)/shard_map/jit(_take)/gather | solution.py:16
  169.5 14.2 %gather_fusion.1 = f32[1024,256,3]{1,2,0:T(4,128)} fusion(f32[256,3,3072]{0,1,2:T(4,128)} %copy.11, s32[1024]{0:T(1024)S(1)} %fusion.12), kind=kCustom, calls=%fused_computation.1.clone | custom fusion | bytes 6295552 | tf_op jit(solution)/shard_map/jit(_take)/gather | solution.py:17
  183.7 9.0 %fusion.1 = f32[256,1024]{0,1:T(8,128)S(1)} fusion(f32[1024,256,3]{1,2,0:T(4,128)} %gather_fusion.1, f32[1024,256,3]{1,2,0:T(4,128)} %gather_fusion, pred[1024]{0:T(1024)(128)(4,1)S(1)} %get-tuple-element.24, pred[1024]{0:T(1024)(128)(4,1)S(1)} %get-tuple-element.25), kind=kLoop, calls=%fused_computation.5 | loop fusion | flops 3670016 | bytes 7342080 | tf_op jit(solution)/shard_map/reduce_sum | solution.py:19
  192.8 1.2 add_sqrt_fusion
  194.1 0.7 fusion.16
  194.8 31.7 %all-gather.2.cloned.1.call-done = f32[512,1024]{0,1:T(8,128)} async-done(((f32[256,1024]{0,1:T(8,128)}), f32[512,1024]{0,1:T(8,128)}) %all-gather.2.cloned.1.call-update) | async-done | bytes 2097168 | tf_op jit(solution)/shard_map/all_gather | solution.py:52
  226.5 1.0 constant_dynamic-slice_fusion
  227.4 1.3 collective-permute-start
  228.7 1.8 multiply_reduce_fusion
  230.6 1.6 dynamic-slice
  232.1 5.1 %collective-permute-done = f32[10,512]{0,1:T(8,128)S(1)} collective-permute-done((f32[10,512]{0,1:T(8,128)S(1)}, f32[10,512]{0,1:T(8,128)S(1)}, u32[]{:S(2)}, u32[]{:S(2)}) %collective-permute-start) | collective-permute-done | bytes 20512 | tf_op jit(solution)/shard_map/ppermute | solution.py:12
  237.5 14.5 %all-reduce.2 = (f32[1024]{0:T(1024)S(1)}, f32[]{:T(128)}, f32[512]{0:T(512)S(1)}) all-reduce(f32[1024]{0:T(1024)S(1)} %multiply_reduce_fusion, f32[]{:T(128)} %get-tuple-element.14, f32[512]{0:T(512)S(1)} %multiply_reduce_fusion.2), channel_id=1, replica_groups=mesh['grp'=2,'atoms'=4,'feat'=2,'rep'=2] {'atoms','rep'}, use_global_device_ids=true, to_apply=%region_2.4 | all-reduce | flops 1537 | bytes 12296 | tf_op jit(solution)/shard_map/psum | solution.py:61
  252.0 0.6 broadcast_divide_fusion.1
  252.5 0.6 broadcast_divide_fusion
  253.1 0.3 multiply_reduce_fusion.1
  253.5 2.1 fusion.2
  255.6 14.1 %all-reduce.1 = (f32[1024]{0:T(1024)S(1)}, f32[512]{0:T(512)S(1)}) all-reduce(f32[1024]{0:T(1024)S(1)} %get-tuple-element.12, f32[512]{0:T(512)S(1)} %get-tuple-element.20), channel_id=1, replica_groups=mesh['grp'=2,'atoms'=4,'feat'=2,'rep'=2] {'atoms','rep'}, use_global_device_ids=true, to_apply=%region_9.11 | all-reduce | flops 1536 | bytes 12288 | tf_op jit(solution)/shard_map/psum | solution.py:75
  269.7 0.6 add_rsqrt_fusion
  270.3 1.1 multiply_bitcast_fusion
  271.4 8.6 %fusion.3 = f32[1024,1024]{1,0:T(8,128)} fusion(f32[512,1024]{0,1:T(8,128)S(1)} %get-tuple-element.13, f32[512,512]{0,1:T(8,128)S(1)} %get-tuple-element.21, f32[512,512]{0,1:T(8,128)S(1)} %get-tuple-element.19), kind=kOutput, calls=%fused_computation.8 | convolution fusion | flops 6442975232 | bytes 8388608 | tf_op jit(solution)/shard_map/dot_general | solution.py:23
  280.1 1.1 copy-done
  281.2 1.3 copy.13
  282.6 0.6 add_rsqrt_fusion.1
  283.1 90.8 %all-reduce.5.cloned.1.call-done = f32[1024,1024]{1,0:T(8,128)} async-done(((f32[1024,1024]{1,0:T(8,128)}), f32[1024,1024]{1,0:T(8,128)}) %all-reduce.5.cloned.1.call-update) | async-done | bytes 4194320 | tf_op jit(solution)/shard_map/psum | solution.py:75
  373.9 2.5 fusion.8
  (16 shorter events, 0.5 us)
Async XLA Ops:
  18.6 6.5 %copy-start.2 = (s32[2,512]{1,0:T(2,128)S(1)}, s32[2,512]{1,0:T(2,128)}, u32[]{:S(2)}) copy-start(s32[2,512]{1,0:T(2,128)} %param.6) | copy-start | bytes 12292
  18.6 111.2 %all-to-all-start = ((bf16[1,4,256,3,768]{2,4,3,0,1:T(8,128)(2,1)}), bf16[1,4,256,3,768]{2,4,3,0,1:T(8,128)(2,1)}, u32[]{:S(2)}, u32[]{:S(2)}) async-start(bf16[1,4,256,3,768]{2,4,3,0,1:T(8,128)(2,1)} %bitcast.23), calls=%async_computation | async-start | bytes 9437184 | tf_op jit(solution)/shard_map/all_to_all | solution.py:47
  25.1 201.4 %all-gather.2.cloned.1.call-start = ((), (), s32[]{:S(2)}) async-start(), calls=%async_computation.1 | async-start | bytes 3145728 | tf_op jit(solution)/shard_map/all_gather | solution.py:52
  183.7 10.4 %copy-start.1 = (s32[1,2048]{1,0:T(1,128)S(1)}, s32[1,2048]{1,0:T(1,128)}, u32[]{:S(2)}) copy-start(s32[1,2048]{1,0:T(1,128)} %param.7) | copy-start | bytes 24580
  194.0 179.9 %all-reduce.5.cloned.1.call-start = ((), (), s32[]{:S(2)}) async-start(), calls=%async_computation.2 | async-start | bytes 8388608 | tf_op jit(solution)/shard_map/psum | solution.py:75
  227.4 9.8 %collective-permute-start = (f32[10,512]{0,1:T(8,128)S(1)}, f32[10,512]{0,1:T(8,128)S(1)}, u32[]{:S(2)}, u32[]{:S(2)}) collective-permute-start(f32[10,512]{0,1:T(8,128)S(1)} %constant_dynamic-slice_fusion), channel_id=1, source_target_pairs={{4,0},{8,4},{12,8},{5,1},{9,5},{13,9},{6,2},{10,6},{14,10},{7,3},{... | collective-permute-start | bytes 61448 | tf_op jit(solution)/shard_map/ppermute | solution.py:12
  280.0 1.2 copy-start
Sparse Core Ops, SparseCore 0:
  194.2 32.2 all-gather.1
  280.2 93.7 all-reduce.4
where the time goes:
time: 384 us; the launch traced here: 383 us
  waiting for transfers between devices  228 us (59%)
  local copies, waits for them, and re-layouts  67.2 us (18%)
  blocking collectives  33 us (9%)
  other arithmetic  24.6 us (6%)
  between operations  14.2 us (4%)
  matrix products  8.59 us (2%)
  starting transfers between devices  7.81 us (2%)
    all_to_all x1, waiting for transfers between devices, shards(): lax.all_to_all(blocks, 'atoms', split_axis=1, concat_axis=4, tiled=True)  100 us
    psum x1, waiting for transfers between devices, shards(): lax.psum((local_moments, spread_now_part, spread_next_part), ('atoms', 'r...  90.8 us
    all_gather x1, waiting for transfers between devices, shards(): every = lax.all_gather(computed, 'feat', axis=0, tiled=True)  31.7 us
    convert_element_type x1, local copies, waits for them, and re-layouts, shards(): lax.all_to_all(blocks, 'atoms', split_axis=1, concat_axis=4, tiled=True)  22.2 us
    psum x1, blocking collectives, shards(): lax.psum((jnp.sum(valid), jnp.sum(valid * every, 0), jnp.sum(valid * futu...  14.5 us
    gather x1, local copies, waits for them, and re-layouts, featurize(): second = jnp.take(positions, pairs[1], axis=2)  14.2 us
    gather x1, local copies, waits for them, and re-layouts, featurize(): first = jnp.take(positions, pairs[0], axis=2)  14.2 us
    psum x1, blocking collectives, shards(): lax.psum((local_moments, spread_now_part, spread_next_part), ('atoms', 'r...  14.1 us
  transfers between devices with their start and end apart: 4, of which 4 were waited for; matrix products, arithmetic and copies ran while one was open for 2% of the time, Pallas kernels for 0%

commit v1 on v0

v1 whole, which is shorter than its diff:
```python
import math

import jax
import jax.numpy as jnp
from jax import lax
from jax.sharding import PartitionSpec as P

LAG = 10


def matmul(left, right, dims, precision=None):
    return lax.dot_general(
        left, right, (dims, ((), ())), precision=precision, preferred_element_type=jnp.float32
    )


def slots_per_pass(width, refs, atoms):
    share = width * (1.0 - math.exp(-refs / atoms)) + 2.05 * math.sqrt(width)
    return min(-(-width // 16) * 16, -(-int(share) // 16) * 16)


def shards(atom_coords, atom_pairs, traj_ids):
    groups = lax.axis_size("atoms")
    feat_groups = lax.axis_size("feat")
    frames = atom_coords.shape[1]
    frames_here = frames // groups
    part = frames_here // feat_groups
    width = atom_coords.shape[3]
    cols = atom_pairs.shape[1]
    z = lax.axis_index("atoms")
    x = lax.axis_index("feat")

    pairs = lax.all_gather(atom_pairs, "feat", axis=1, tiled=True)
    feats = pairs.shape[1]
    refs = pairs.reshape(-1)
    room = slots_per_pass(width, 2 * feats, width * groups)

    atom_no = jnp.arange(groups * width, dtype=jnp.int32).reshape(groups, width)
    hit = atom_no[:, :, None] == refs[None, None, :]
    used = jnp.any(hit, axis=2)
    before = (jnp.arange(width)[:, None] < jnp.arange(width)[None, :]).astype(jnp.bfloat16)
    rank = matmul(used.astype(jnp.bfloat16), before, ((1,), (0,)))
    most = jnp.max(jnp.sum(used.astype(jnp.float32), 1))
    ref_rank = jnp.sum(jnp.where(hit, rank[:, :, None], 0.0), axis=(0, 1)).reshape(2, feats)
    ref_shard = pairs // width
    used_own = lax.dynamic_index_in_dim(used, z, 0, False)
    rank_own = lax.dynamic_index_in_dim(rank, z, 0, False)

    grouped = jnp.transpose(atom_coords[0], (1, 0, 2)).reshape(3, groups, feat_groups, part, width)
    blocks = lax.dynamic_index_in_dim(grouped, x, 2, False)

    def deltas(turn):
        first = turn * jnp.float32(room)
        slot = jnp.arange(room, dtype=jnp.float32) + first
        pick = ((rank_own[None, :] == slot[:, None]) & used_own[None, :]).astype(jnp.bfloat16)
        chosen = lax.dot_general(
            pick, blocks, (((1,), (3,)), ((), ())), preferred_element_type=jnp.float32
        ).astype(jnp.bfloat16)
        chosen = jnp.transpose(chosen, (2, 1, 0, 3))
        got = lax.all_to_all(chosen, "atoms", split_axis=0, concat_axis=0, tiled=True)
        shard_no = jnp.arange(groups, dtype=jnp.int32)
        place = (ref_rank[:, None, :, None] == slot) & (ref_shard[:, None, :, None] == shard_no[:, None, None])
        sign = place[0].astype(jnp.bfloat16) - place[1].astype(jnp.bfloat16)
        total = 0.0
        for s in range(groups):
            total = total + lax.dot_general(
                sign[s], got[s], (((1,), (1,)), ((), ())), preferred_element_type=jnp.float32
            )
        return total

    delta = deltas(jnp.float32(0.0))
    _, delta = lax.while_loop(
        lambda c: c[0] * room < most, lambda c: (c[0] + 1.0, c[1] + deltas(c[0])), (jnp.float32(1.0), delta)
    )
    computed = jnp.sqrt(jnp.sum(delta * delta, axis=1) + 0.01).T

    every = lax.all_gather(computed, "feat", axis=0, tiled=True)
    own = lax.dynamic_slice_in_dim(every, x * cols, cols, 1)
    route = [(i, i - 1) for i in range(1, groups)]
    incoming = lax.ppermute(own[:LAG], "atoms", route)
    future = jnp.concatenate([own[LAG:], incoming], 0)

    ids = jnp.concatenate([traj_ids[0], jnp.full((LAG,), -1, jnp.int32)])
    ids_now = lax.dynamic_slice_in_dim(ids, z * frames_here, frames_here)
    ids_later = lax.dynamic_slice_in_dim(ids, z * frames_here + LAG, frames_here)
    valid = (ids_now == ids_later).astype(jnp.float32)[:, None]

    count_b = jnp.sum(valid)
    inverse = 1.0 / jnp.maximum(count_b, 1.0)
    now_b = jnp.sum(valid * every, 0) * inverse
    next_b = jnp.sum(valid * future, 0) * inverse
    now_c = valid * (every - now_b)
    next_c = valid * (future - next_b)
    own_c = lax.dynamic_slice_in_dim(now_c, x * cols, cols, 1)
    stats = jnp.concatenate(
        [now_b, next_b, jnp.sum(now_c * now_c, 0), jnp.sum(next_c * next_c, 0), jnp.full((128,), count_b)]
    )
    stats = lax.all_gather(stats, ("atoms", "rep"), axis=0, tiled=False)

    local = matmul(now_c, jnp.concatenate([own_c, next_c], 1), ((0,), (0,)), lax.Precision.HIGH)
    mine = lax.psum_scatter(local, ("atoms", "rep"), scatter_dimension=0, tiled=True)

    counts = stats[:, -1:]
    now_all = stats[:, :feats]
    next_all = stats[:, feats : feats + cols]
    sq_now = stats[:, feats + cols : 2 * feats + cols]
    sq_next = stats[:, 2 * feats + cols : 2 * feats + 2 * cols]
    count = jnp.sum(counts)
    mean_now = jnp.sum(counts * now_all, 0) / count
    mean_next = jnp.sum(counts * next_all, 0) / count
    off_now = now_all - mean_now
    off_next = next_all - mean_next
    spread_now = jnp.sum(sq_now + counts * off_now * off_now, 0)
    spread_next = jnp.sum(sq_next + counts * off_next * off_next, 0)
    scale_now = 1.0 / jnp.sqrt(spread_now / count + 1e-05)
    scale_next = 1.0 / jnp.sqrt(spread_next / count + 1e-05)

    rows = feats // lax.axis_size(("atoms", "rep"))
    row = lax.axis_index(("atoms", "rep")) * rows
    off_rows = lax.dynamic_slice_in_dim(off_now, row, rows, 1)
    off_cols = lax.dynamic_slice_in_dim(off_now, x * cols, cols, 1)
    mine = mine + matmul(
        counts * off_rows, jnp.concatenate([off_cols, off_next], 1), ((0,), (0,)), lax.Precision.HIGHEST
    )
    scale_rows = lax.dynamic_slice_in_dim(scale_now, row, rows)
    scale_cols = lax.dynamic_slice_in_dim(scale_now, x * cols, cols)
    mean_cols = lax.dynamic_slice_in_dim(mean_now, x * cols, cols)
    corr_inst = mine[:, :cols] / count * scale_rows[:, None] * scale_cols[None, :]
    corr_lag = mine[:, cols:] / count * scale_rows[:, None] * scale_next[None, :]
    projections = ((own - mean_cols) * scale_cols)[None]
    return (corr_inst, corr_lag, projections)


def solution(mesh):
    placed = (P(("grp", "rep"), None, None, "atoms"), P(None, "feat"), P(("grp", "rep"), None))
    return jax.shard_map(
        shards,
        mesh=mesh,
        in_specs=placed,
        out_specs=(
            P(("grp", "atoms", "rep"), "feat"),
            P(("grp", "atoms", "rep"), "feat"),
            P(("grp", "rep"), "atoms", "feat"),
        ),
        check_vma=False,
    )
```

time: 384 us -> 209 us (0.54)
  waiting for transfers between devices: 228 us -> 117 us
  local copies, waits for them, and re-layouts: 67.2 us -> 8.29 us
  blocking collectives: 33 us -> 20 us
  matrix products: 8.59 us -> 18.5 us
    psum x1 -> x0, waiting for transfers between devices: 90.8 us -> none  [shards(): lax.psum((local_moments, spread_now_part, spread_next_part), ('atoms', 'r...]
    all_to_all x1, waiting for transfers between devices: 100 us -> 51.6 us  [deltas(): lax.all_to_all(chosen, 'atoms', split_axis=0, concat_axis=0, tiled=True)]
    reduce_scatter x0 -> x1, waiting for transfers between devices: none -> 29.3 us  [shards(): lax.psum_scatter(local, ('atoms', 'rep'), scatter_dimension=0, tiled=True)]
    psum x2 -> x0, blocking collectives: 28.6 us -> none  [the longest x1 14.5 us: shards(): lax.psum((jnp.sum(valid), jnp.sum(valid * every, 0), jnp.sum(valid * futu...]
    gather x2 -> x0, local copies, waits for them, and re-layouts: 28.4 us -> none  [the longest x1 14.2 us: featurize(): second = jnp.take(positions, pairs[1], axis=2)]
    convert_element_type x1, local copies, waits for them, and re-layouts: 22.2 us -> 1.75 us  [deltas(): chosen = lax.dot_general(pick, blocks, (((1,), (3,)), ((), ())), preferre...]
    all_gather x1 -> x2, blocking collectives: 4.36 us -> 20 us  [the longest x1 14.5 us: shards(): stats = lax.all_gather(stats, ('atoms', 'rep'), axis=0, tiled=False)]
    dot_general x1 -> x8, matrix products: 8.59 us -> 18.5 us  [the longest x4 8.86 us: deltas(): lax.dot_general(sign[s], got[s], (((1,), (1,)), ((), ())), preferred_elem...]
  transfers between devices with their start and end apart: 4 -> 4, of which waited for: 4 -> 4; matrix products, arithmetic and copies ran while one was open for 2% -> 8% of each run, Pallas kernels for 0% -> 0%
where the time goes in v1:
time: 209 us; the launch traced here: 208 us
  waiting for transfers between devices  117 us (56%)
  other arithmetic  21 us (10%)
  blocking collectives  20 us (10%)
  matrix products  18.5 us (9%)
  between operations  15.1 us (7%)
  local copies, waits for them, and re-layouts  8.29 us (4%)
  starting transfers between devices  6.95 us (3%)
    all_to_all x1, waiting for transfers between devices, deltas(): lax.all_to_all(chosen, 'atoms', split_axis=0, concat_axis=0, tiled=True)  51.6 us
    all_gather x1, waiting for transfers between devices, shards(): every = lax.all_gather(computed, 'feat', axis=0, tiled=True)  30.9 us
    reduce_scatter x1, waiting for transfers between devices, shards(): lax.psum_scatter(local, ('atoms', 'rep'), scatter_dimension=0, tiled=True)  29.3 us
    all_gather x1, blocking collectives, shards(): stats = lax.all_gather(stats, ('atoms', 'rep'), axis=0, tiled=False)  14.5 us
    dot_general x4, matrix products, deltas(): lax.dot_general(sign[s], got[s], (((1,), (1,)), ((), ())), preferred_elem...  8.86 us
    dot_general x3, matrix products, matmul(): lax.dot_general(left, right, (dims, ((), ())), precision=precision, prefe...  7.28 us
    all_gather x1, blocking collectives, shards(): pairs = lax.all_gather(atom_pairs, 'feat', axis=1, tiled=True)  5.49 us
    ppermute x1, waiting for transfers between devices, shards(): incoming = lax.ppermute(own[:LAG], 'atoms', route)  5.44 us
  transfers between devices with their start and end apart: 4, of which 4 were waited for; matrix products, arithmetic and copies ran while one was open for 8% of the time, Pallas kernels for 0%

profile of v1, /device:TPU:0, one launch (start us, length us, event | category | flops | bytes accessed | tf_op | source)
XLA Modules:
  0.0 207.9 jit_solution(13706611809505644182)
XLA Ops:
  7.2 5.5 %all_gather.12 = s32[2,1024]{1,0:T(2,128)S(1)} all-gather(s32[2,512]{1,0:T(2,128)} %param.6), channel_id=1, replica_groups=mesh['grp'=2,'atoms'=4,'feat'=2,'rep'=2] {'feat'}, dimensions={1}, use_global_device_ids=true | all-gather | bytes 12288 | tf_op jit(solution)/shard_map/all_gather | solution.py:33
  12.7 3.7 %compare_reduce_fusion = pred[4,768]{1,0:T(4,128)(4,1)S(1)} fusion(s32[2048]{0:T(1024)S(1)} %bitcast.144, s32[4,768]{1,0:T(4,128)S(1)} %multiply_add_fusion), kind=kLoop, calls=%fused_computation.27 | loop fusion | flops 12579840 | bytes 23552 | tf_op jit(solution)/shard_map/reduce_or | solution.py:40
  16.7 2.6 %dynamic-slice_bitcast_fusion = bf16[3,4,256,768]{3,2,1,0:T(8,128)(2,1)S(1)} fusion(bf16[3,4,2,256,768]{4,3,2,1,0:T(8,128)(2,1)} %bitcast.136, s32[]{:T(128)S(6)} %select_n.41), kind=kLoop, calls=%fused_computation.32 | loop fusion | bytes 9437188 | tf_op jit(solution)/shard_map/jit(dynamic_index_in_dim)/squeeze | solution.py:50
  19.4 2.3 %convert_bitcast_fusion.1 = bf16[4,3,432,256]{3,2,0,1:T(8,128)(2,1)S(1)} fusion(bf16[3,4,256,768]{3,2,1,0:T(8,128)(2,1)S(1)} %dynamic-slice_bitcast_fusion, f32[768]{0:T(1024)S(1)} %dynamic-slice_reduce_fusion.1, pred[768]{0:T(1024)(128)(4,1)S(1)} %dynamic-slice_reduce_fusion), kind=kOutput, calls=%fused_computation.37 | convolution fusion | flops 2040422400 | bytes 7376640 | tf_op jit(solution)/shard_map/dot_general | solution.py:56
  21.7 1.8 copy.15
  23.4 5.3 %all-to-all-start.1 = ((bf16[4,3,432,256]{3,2,1,0:T(8,128)(2,1)}), bf16[4,3,432,256]{3,2,1,0:T(8,128)(2,1)}, u32[]{:S(2)}, u32[]{:S(2)}) async-start(bf16[4,3,432,256]{3,2,1,0:T(8,128)(2,1)} %copy.15), calls=%async_computation.1 | async-start | bytes 5308416 | tf_op jit(solution)/shard_map/all_to_all | solution.py:60
  28.8 3.0 %fusion.10 = f32[2048]{0:T(1024)S(1)} fusion(f32[4,768]{1,0:T(4,128)S(1)} %fusion.12, s32[2048]{0:T(1024)S(1)} %bitcast.145, s32[4,768]{1,0:T(4,128)S(1)} %multiply_add_fusion), kind=kLoop, calls=%fused_computation.28 | loop fusion | flops 18872320 | bytes 40960 | tf_op jit(solution)/shard_map/reduce_sum | solution.py:44
  31.9 0.6 reduce_max.9
  33.1 1.7 broadcast_and_fusion.1
  34.8 1.5 fusion.11
  36.3 51.6 %all-to-all-done.1 = bf16[4,3,432,256]{3,2,1,0:T(8,128)(2,1)} async-done(((bf16[4,3,432,256]{3,2,1,0:T(8,128)(2,1)}), bf16[4,3,432,256]{3,2,1,0:T(8,128)(2,1)}, u32[]{:S(2)}, u32[]{:S(2)}) %all-to-all-start.1) | async-done | bytes 2654240 | tf_op jit(solution)/shard_map/all_to_all | solution.py:60
  87.9 2.1 %fusion.21 = f32[1024,3,256]{2,0,1:T(8,128)S(1)} fusion(bf16[1,4,1024,432]{2,3,1,0:T(8,128)(2,1)S(1)} %fusion.11, bf16[4,3,432,256]{3,2,1,0:T(8,128)(2,1)} %all-to-all-done.1), kind=kOutput, calls=%fused_computation.61 | convolution fusion | flops 679477248 | bytes 4694016 | tf_op jit(solution)/shard_map/dot_general | solution.py:66
  90.0 2.1 %fusion.22 = f32[1024,3,256]{2,0,1:T(8,128)S(1)} fusion(bf16[1,4,1024,432]{2,3,1,0:T(8,128)(2,1)S(1)} %fusion.11, bf16[4,3,432,256]{3,2,1,0:T(8,128)(2,1)} %all-to-all-done.1), kind=kOutput, calls=%fused_computation.63 | convolution fusion | flops 679477248 | bytes 4694016 | tf_op jit(solution)/shard_map/dot_general | solution.py:66
  92.1 2.1 %fusion.20 = f32[1024,3,256]{2,0,1:T(8,128)S(1)} fusion(bf16[1,4,1024,432]{2,3,1,0:T(8,128)(2,1)S(1)} %fusion.11, bf16[4,3,432,256]{3,2,1,0:T(8,128)(2,1)} %all-to-all-done.1), kind=kOutput, calls=%fused_computation.59 | convolution fusion | flops 679477248 | bytes 4694016 | tf_op jit(solution)/shard_map/dot_general | solution.py:66
  94.2 2.5 %add_add_fusion.1 = f32[1024,3,256]{2,0,1:T(8,128)S(1)} fusion(f32[1024,3,256]{2,0,1:T(8,128)S(1)} %fusion.20, f32[1024,3,256]{2,0,1:T(8,128)S(1)} %fusion.22, f32[1024,3,256]{2,0,1:T(8,128)S(1)} %fusion.21, bf16[1,4,1024,432]{2,3,1,0:T(8,128)(2,1)} %copy-done.2, bf16[4,3,432,256]{3,2,1,0:T(8,128)(2,1)} %all-to-all-done.1), kind=kOutput, calls=%fused_computation.36 | convolution fusion | flops 681836544 | bytes 14131200 | tf_op jit(solution)/shard_map/dot_general | solution.py:66
  96.8 0.8 while.11
  97.9 1.2 sqrt_bitcast_fusion
  99.2 0.7 fusion.44
  100.6 30.9 %all-gather.4.cloned.1.call-done = f32[512,1024]{0,1:T(8,128)} async-done(((f32[256,1024]{0,1:T(8,128)}), f32[512,1024]{0,1:T(8,128)}) %all-gather.4.cloned.1.call-update) | async-done | bytes 2097168 | tf_op jit(solution)/shard_map/all_gather | solution.py:77
  131.5 1.1 constant_dynamic-slice_fusion
  132.6 1.6 collective-permute-start
  134.2 1.8 multiply_reduce_fusion.2
  137.0 5.4 %collective-permute-done = f32[10,512]{0,1:T(8,128)S(1)} collective-permute-done((f32[10,512]{0,1:T(8,128)S(1)}, f32[10,512]{0,1:T(8,128)S(1)}, u32[]{:S(2)}, u32[]{:S(2)}) %collective-permute-start) | collective-permute-done | bytes 20512 | tf_op jit(solution)/shard_map/ppermute | solution.py:80
  143.0 5.3 %fusion.13 = f32[1024,1024]{1,0:T(8,128)} fusion(f32[512,1024]{0,1:T(8,128)S(1)} %get-tuple-element.78, f32[512,512]{0,1:T(8,128)S(1)} %get-tuple-element.76, f32[512,512]{0,1:T(8,128)S(1)} %constant_dynamic-slice_fusion.2), kind=kOutput, calls=%fused_computation.40 | convolution fusion | flops 3221749760 | bytes 8388608 | tf_op jit(solution)/shard_map/dot_general | solution.py:12
  148.4 0.6 constant_dynamic-update-slice_fusion
  149.1 14.5 %all-gather.1 = f32[8,1,3200]{2,1,0:T(1,128)S(1)} all-gather(f32[1,1,3200]{2,1,0:T(1,128)S(1)} %reshape.107), channel_id=2, replica_groups=mesh['grp'=2,'atoms'=4,'feat'=2,'rep'=2] {'atoms','rep'}, dimensions={0}, use_global_device_ids=true | all-gather | bytes 115200 | tf_op jit(solution)/shard_map/all_gather | solution.py:98
  163.6 0.6 slice_reduce_fusion
  165.1 0.6 add_rsqrt_fusion
  165.9 1.3 copy.16
  168.6 29.3 %reduce-scatter.2.cloned.1.call-done = f32[128,1024]{1,0:T(8,128)} async-done(((f32[1024,1024]{1,0:T(8,128)}), f32[128,1024]{1,0:T(8,128)}) %reduce-scatter.2.cloned.1.call-update) | async-done | bytes 524304 | tf_op jit(solution)/shard_map/reduce_scatter | solution.py:101
  197.9 1.7 convolution_add_fusion
  199.6 1.4 fusion.26
  (56 shorter events, 5.3 us)
Async XLA Ops:
  16.6 2.7 %copy-start.8 = (pred[768]{0:T(1024)(128)(4,1)}, pred[768]{0:T(1024)(128)(4,1)S(1)}, u32[]{:S(2)}) copy-start(pred[768]{0:T(1024)(128)(4,1)S(1)} %dynamic-slice_reduce_fusion) | copy-start | bytes 2308
  16.7 2.7 %copy-start.6 = (f32[768]{0:T(1024)}, f32[768]{0:T(1024)S(1)}, u32[]{:S(2)}) copy-start(f32[768]{0:T(1024)S(1)} %dynamic-slice_reduce_fusion.1) | copy-start | bytes 9220
  19.3 2.3 %copy-start.3 = (bf16[3,4,256,768]{3,2,1,0:T(8,128)(2,1)}, bf16[3,4,256,768]{3,2,1,0:T(8,128)(2,1)S(1)}, u32[]{:S(2)}) copy-start(bf16[3,4,256,768]{3,2,1,0:T(8,128)(2,1)S(1)} %dynamic-slice_bitcast_fusion) | copy-start | bytes 14155780
  23.4 64.4 %all-to-all-start.1 = ((bf16[4,3,432,256]{3,2,1,0:T(8,128)(2,1)}), bf16[4,3,432,256]{3,2,1,0:T(8,128)(2,1)}, u32[]{:S(2)}, u32[]{:S(2)}) async-start(bf16[4,3,432,256]{3,2,1,0:T(8,128)(2,1)} %copy.15), calls=%async_computation.1 | async-start | bytes 5308416 | tf_op jit(solution)/shard_map/all_to_all | solution.py:60
  28.8 102.7 %all-gather.4.cloned.1.call-start = ((), (), s32[]{:S(2)}) async-start(), calls=%async_computation.3 | async-start | bytes 3145728 | tf_op jit(solution)/shard_map/all_gather | solution.py:77
  31.8 0.8 copy-start.4
  36.3 55.8 %copy-start.2 = (bf16[1,4,1024,432]{2,3,1,0:T(8,128)(2,1)}, bf16[1,4,1024,432]{2,3,1,0:T(8,128)(2,1)S(1)}, u32[]{:S(2)}) copy-start(bf16[1,4,1024,432]{2,3,1,0:T(8,128)(2,1)S(1)} %fusion.11) | copy-start | bytes 10616836
  94.2 2.6 %copy-start.7 = (f32[768]{0:T(1024)S(1)}, f32[768]{0:T(1024)}, u32[]{:S(2)}) copy-start(f32[768]{0:T(1024)} %copy-done.6) | copy-start | bytes 9220
  94.2 2.6 %copy-start.9 = (pred[768]{0:T(1024)(128)(4,1)S(1)}, pred[768]{0:T(1024)(128)(4,1)}, u32[]{:S(2)}) copy-start(pred[768]{0:T(1024)(128)(4,1)} %copy-done.8) | copy-start | bytes 2308
  97.6 1.6 copy-start.5
  99.2 98.8 %reduce-scatter.2.cloned.1.call-start = ((), (), s32[]{:S(2)}) async-start(), calls=%async_computation.4 | async-start | bytes 4718592 | tf_op jit(solution)/shard_map/reduce_scatter | solution.py:101
  131.5 4.5 %copy-start.1 = (f32[512,1024]{0,1:T(8,128)S(1)}, f32[512,1024]{0,1:T(8,128)}, u32[]{:S(2)}) copy-start(f32[512,1024]{0,1:T(8,128)} %all-gather.4.cloned.1.call-done) | copy-start | bytes 6291460
  132.6 9.8 %collective-permute-start = (f32[10,512]{0,1:T(8,128)S(1)}, f32[10,512]{0,1:T(8,128)S(1)}, u32[]{:S(2)}, u32[]{:S(2)}) collective-permute-start(f32[10,512]{0,1:T(8,128)S(1)} %constant_dynamic-slice_fusion), channel_id=1, source_target_pairs={{4,0},{8,4},{12,8},{5,1},{9,5},{13,9},{6,2},{10,6},{14,10},{7,3},{... | collective-permute-start | bytes 61448 | tf_op jit(solution)/shard_map/ppermute | solution.py:80
Sparse Core Ops, SparseCore 0:
  99.3 32.1 all-gather.3
  148.5 49.3 reduce-scatter.1

commit v2 on v1

--- a/solution.py
+++ b/solution.py
@@ -1,8 +1,11 @@
+import functools
 import math
 
 import jax
 import jax.numpy as jnp
 from jax import lax
+from jax.experimental import pallas as pl
+from jax.experimental.pallas import tpu as pltpu
 from jax.sharding import PartitionSpec as P
 
 LAG = 10
@@ -12,6 +15,126 @@
     return lax.dot_general(
         left, right, (dims, ((), ())), precision=precision, preferred_element_type=jnp.float32
     )
+
+MESH = pl.DeviceIdType.MESH
+
+
+def exchange_kernel(groups, feat_groups, room, lanes, chunks, tile, chosen, slots, out, sign, recv, *sems):
+    z_send, z_recv, z_own, x_send, x_recv = sems
+    z, x = lax.axis_index("atoms"), lax.axis_index("feat")
+    half = groups // 2
+    z_steps = [half] + [o for o in range(groups - 1, 0, -1) if o != half] if groups > 1 else []
+    x_steps = list(range(1, feat_groups))
+    tiles = out.shape[0] // tile
+    barrier = pltpu.get_barrier_semaphore()
+    for o in z_steps:
+        pl.semaphore_signal(barrier, 1, device_id={"atoms": lax.rem(z + o, groups)}, device_id_type=MESH)
+    for o in x_steps:
+        pl.semaphore_signal(barrier, 1, device_id={"feat": lax.rem(x + o, feat_groups)}, device_id_type=MESH)
+    pl.semaphore_wait(barrier, len(z_steps) + len(x_steps))
+
+    here = pl.ds(pl.multiple_of(z * room, 16), room)
+    z_copies = []
+    for ch in range(chunks):
+        row = []
+        for i, o in enumerate(z_steps):
+            dest = lax.rem(z + o, groups)
+            row.append(
+                pltpu.make_async_remote_copy(
+                    src_ref=chosen.at[dest, ch],
+                    dst_ref=recv.at[ch, here],
+                    send_sem=z_send.at[ch, i],
+                    recv_sem=z_recv.at[ch, i],
+                    device_id={"atoms": dest},
+                    device_id_type=MESH,
+                )
+            )
+            row[-1].start()
+        z_copies.append(row)
+    own_copies = [pltpu.make_async_copy(chosen.at[z, ch], recv.at[ch, here], z_own.at[ch]) for ch in range(chunks)]
+    for copy in own_copies:
+        copy.start()
+
+    place = lax.broadcasted_iota(jnp.int32, (128, groups * room), 1)
+
+    def make_sign(i, carry):
+        rows = pl.ds(pl.multiple_of(i * 128, 128), 128)
+        pair = slots[rows, :]
+        value = jnp.where(place == pair[:, 0:1], 1.0, 0.0) - jnp.where(place == pair[:, 1:2], 1.0, 0.0)
+        sign[rows, :] = value.astype(jnp.bfloat16)
+        return carry
+
+    lax.fori_loop(0, out.shape[0] // 128, make_sign, 0)
+
+    def x_copy(ch, i, k, o):
+        part = out.at[
+            pl.ds(pl.multiple_of(i * tile, tile), tile),
+            pl.ds(pl.multiple_of((x * chunks + ch) * lanes, lanes), lanes),
+        ]
+        return pltpu.make_async_remote_copy(
+            src_ref=part,
+            dst_ref=part,
+            send_sem=x_send.at[ch, i, k],
+            recv_sem=x_recv.at[ch, i, k],
+            device_id={"feat": lax.rem(x + o, feat_groups)},
+            device_id_type=MESH,
+        )
+
+    for ch in range(chunks):
+        own_copies[ch].wait()
+        for copy in z_copies[ch]:
+            copy.wait_recv()
+
+        def features(i, carry, ch=ch):
+            rows = pl.ds(pl.multiple_of(i * tile, tile), tile)
+            delta = jnp.dot(sign[rows, :], recv[ch], preferred_element_type=jnp.float32)
+            square = delta * delta
+            total = square[:, :lanes] + square[:, lanes : 2 * lanes] + square[:, 2 * lanes :]
+            cols = pl.ds(pl.multiple_of((x * chunks + ch) * lanes, lanes), lanes)
+            out[rows, cols] = jnp.sqrt(total + 0.01)
+            for k, o in enumerate(x_steps):
+                x_copy(ch, i, k, o).start()
+            return carry
+
+        lax.fori_loop(0, tiles, features, 0)
+
+    for ch in range(chunks):
+        for copy in z_copies[ch]:
+            copy.wait_send()
+
+        def finish(i, carry, ch=ch):
+            for k, o in enumerate(x_steps):
+                x_copy(ch, i, k, o).wait()
+            return carry
+
+        lax.fori_loop(0, tiles, finish, 0)
+
+
+def exchange(chosen, slots, groups, feat_groups):
+    chunks, room, lanes = chosen.shape[1], chosen.shape[2], chosen.shape[3] // 3
+    feats = slots.shape[0]
+    tile = min(256, feats)
+    vmem = pl.BlockSpec(memory_space=pltpu.VMEM)
+    z_count, x_count = max(groups - 1, 1), max(feat_groups - 1, 1)
+    dma = pltpu.SemaphoreType.DMA
+    return pl.pallas_call(
+        functools.partial(exchange_kernel, groups, feat_groups, room, lanes, chunks, tile),
+        out_shape=jax.ShapeDtypeStruct((feats, feat_groups * chunks * lanes), jnp.float32),
+        in_specs=[vmem, vmem],
+        out_specs=vmem,
+        scratch_shapes=[
+            pltpu.VMEM((feats, groups * room), jnp.bfloat16),
+            pltpu.VMEM((chunks, groups * room, 3 * lanes), jnp.bfloat16),
+            dma((chunks, z_count)),
+            dma((chunks, z_count)),
+            dma((chunks,)),
+            dma((chunks, feats // tile, x_count)),
+            dma((chunks, feats // tile, x_count)),
+        ],
+        compiler_params=pltpu.CompilerParams(
+            collective_id=0, has_side_effects=True, vmem_limit_bytes=48 * 1024 * 1024
+        ),
+    )(chosen, slots)
 
 
 def slots_per_pass(width, refs, atoms):
@@ -49,32 +172,44 @@
     grouped = jnp.transpose(atom_coords[0], (1, 0, 2)).reshape(3, groups, feat_groups, part, width)
     blocks = lax.dynamic_index_in_dim(grouped, x, 2, False)
 
-    def deltas(turn):
-        first = turn * jnp.float32(room)
-        slot = jnp.arange(room, dtype=jnp.float32) + first
+    lanes = 128 if part % 128 == 0 else part
+    chunks = part // lanes
+
+    def select(turn):
+        slot = jnp.arange(room, dtype=jnp.float32) + turn * jnp.float32(room)
         pick = ((rank_own[None, :] == slot[:, None]) & used_own[None, :]).astype(jnp.bfloat16)
         chosen = lax.dot_general(
             pick, blocks, (((1,), (3,)), ((), ())), preferred_element_type=jnp.float32
         ).astype(jnp.bfloat16)
-        chosen = jnp.transpose(chosen, (2, 1, 0, 3))
-        got = lax.all_to_all(chosen, "atoms", split_axis=0, concat_axis=0, tiled=True)
-        shard_no = jnp.arange(groups, dtype=jnp.int32)
-        place = (ref_rank[:, None, :, None] == slot) & (ref_shard[:, None, :, None] == shard_no[:, None, None])
-        sign = place[0].astype(jnp.bfloat16) - place[1].astype(jnp.bfloat16)
-        total = 0.0
-        for s in range(groups):
-            total = total + lax.dot_general(
-                sign[s], got[s], (((1,), (1,)), ((), ())), preferred_element_type=jnp.float32
-            )
-        return total
-
-    delta = deltas(jnp.float32(0.0))
-    _, delta = lax.while_loop(
-        lambda c: c[0] * room < most, lambda c: (c[0] + 1.0, c[1] + deltas(c[0])), (jnp.float32(1.0), delta)
-    )
-    computed = jnp.sqrt(jnp.sum(delta * delta, axis=1) + 0.01).T
-
-    every = lax.all_gather(computed, "feat", axis=0, tiled=True)
+        chosen = jnp.transpose(chosen.reshape(room, 3, groups, chunks, lanes), (2, 3, 0, 1, 4))
+        spot = ref_rank - turn * jnp.float32(room)
+        inside = (spot >= 0) & (spot < room)
+        spot = jnp.where(inside, ref_shard * room + spot.astype(jnp.int32), -1)
+        return chosen.reshape(groups, chunks, room, 3 * lanes), spot.T
+
+    def one_pass():
+        return exchange(*select(jnp.float32(0.0)), groups, feat_groups)
+
+    def more_passes():
+        def step(carry):
+            turn, delta = carry
+            chosen, spot = select(turn)
+            got = lax.all_to_all(chosen, "atoms", split_axis=0, concat_axis=0, tiled=True)
+            got = jnp.transpose(got, (0, 2, 1, 3)).reshape(groups * room, chunks * 3 * lanes)
+            place = jnp.arange(groups * room, dtype=jnp.int32)
+            sign = (spot[:, :1] == place).astype(jnp.bfloat16) - (spot[:, 1:] == place).astype(jnp.bfloat16)
+            return turn + 1.0, delta + matmul(sign, got, ((1,), (0,)))
+
+        _, delta = lax.while_loop(
+            lambda c: c[0] * room < most,
+            step,
+            (jnp.float32(0.0), jnp.zeros((feats, chunks * 3 * lanes), jnp.float32)),
+        )
+        delta = delta.reshape(feats, chunks, 3, lanes)
+        computed = jnp.sqrt(jnp.sum(delta * delta, axis=2) + 0.01).reshape(feats, part)
+        return lax.all_gather(computed, "feat", axis=1, tiled=True)
+
+    every = lax.cond(most <= room, one_pass, more_passes).T
     own = lax.dynamic_slice_in_dim(every, x * cols, cols, 1)
     route = [(i, i - 1) for i in range(1, groups)]
     incoming = lax.ppermute(own[:LAG], "atoms", route)

time: 209 us -> 205 us (0.981)
  waiting for transfers between devices: 117 us -> 37.2 us
  Pallas kernels: 0 us -> 68.3 us
  local copies, waits for them, and re-layouts: 8.29 us -> 26.3 us
  starting transfers between devices: 6.95 us -> 1.34 us
  matrix products: 18.5 us -> 13.2 us
  other arithmetic: 21 us -> 16.5 us
  blocking collectives: 20 us -> 24.4 us
    pallas_call x0 -> x1, Pallas kernels: none -> 68.3 us  [exchange(): pl.pallas_call(functools.partial(exchange_kernel, groups, feat_groups, ro...]
    all_to_all x1 -> x0, waiting for transfers between devices: 51.6 us -> none  [deltas(): lax.all_to_all(chosen, 'atoms', split_axis=0, concat_axis=0, tiled=True)]
    all_gather x1 -> x0, waiting for transfers between devices: 30.9 us -> none  [shards(): every = lax.all_gather(computed, 'feat', axis=0, tiled=True)]
    reshape x0 -> x4, local copies, waits for them, and re-layouts: none -> 14.1 us  [the longest x2 10.6 us: select(): chosen.reshape(room, 3, groups, chunks, lanes)]
    all_to_all x1 -> x0, starting transfers between devices: 5.35 us -> none  [deltas(): lax.all_to_all(chosen, 'atoms', split_axis=0, concat_axis=0, tiled=True)]
    dot_general x5 -> x1, matrix products: 11.2 us -> 6.13 us  [select(): lax.dot_general(pick, blocks, (((1,), (3,)), ((), ())), preferred_element...]
    all_gather x1, blocking collectives: 5.49 us -> 9.94 us  [shards(): pairs = lax.all_gather(atom_pairs, 'feat', axis=1, tiled=True)]
    cond x0 -> x7, local copies, waits for them, and re-layouts: none -> 4.09 us
  transfers between devices with their start and end apart: 4 -> 2, of which waited for: 4 -> 2; matrix products, arithmetic and copies ran while one was open for 8% -> 3% of each run, Pallas kernels for 0% -> 0%
where the time goes in v2:
time: 205 us
  Pallas kernels  68.3 us (33%)
  waiting for transfers between devices  37.2 us (18%)
  local copies, waits for them, and re-layouts  26.3 us (13%)
  blocking collectives  24.4 us (12%)
  between operations  17 us (8%)
  other arithmetic  16.5 us (8%)
  matrix products  13.2 us (6%)
    pallas_call x1, Pallas kernels, exchange(): pl.pallas_call(functools.partial(exchange_kernel, groups, feat_groups, ro...  68.3 us
    reduce_scatter x1, waiting for transfers between devices, shards(): lax.psum_scatter(local, ('atoms', 'rep'), scatter_dimension=0, tiled=True)  29.2 us
    all_gather x1, blocking collectives, shards(): stats = lax.all_gather(stats, ('atoms', 'rep'), axis=0, tiled=False)  14.5 us
    reshape x2, local copies, waits for them, and re-layouts, select(): chosen.reshape(room, 3, groups, chunks, lanes)  10.6 us
    all_gather x1, blocking collectives, shards(): pairs = lax.all_gather(atom_pairs, 'feat', axis=1, tiled=True)  9.94 us
    ppermute x1, waiting for transfers between devices, shards(): incoming = lax.ppermute(own[:LAG], 'atoms', route)  7.96 us
    dot_general x3, matrix products, matmul(): lax.dot_general(left, right, (dims, ((), ())), precision=precision, prefe...  7.09 us
    dot_general x1, matrix products, select(): lax.dot_general(pick, blocks, (((1,), (3,)), ((), ())), preferred_element...  6.13 us
  transfers between devices with their start and end apart: 2, of which 2 were waited for; matrix products, arithmetic and copies ran while one was open for 3% of the time, Pallas kernels for 0%

profile of v2, /device:TPU:0, one launch (start us, length us, event | category | flops | bytes accessed | tf_op | source)
XLA Modules:
  0.0 204.7 jit_solution(5721195559251001567)
XLA Ops:
  8.0 0.8 copy.66
  8.9 9.9 %all_gather.12 = s32[2,1024]{0,1:T(8,128)S(1)} all-gather(s32[2,512]{0,1:T(8,128)S(1)} %copy.66), channel_id=1, replica_groups=mesh['grp'=2,'atoms'=4,'feat'=2,'rep'=2] {'feat'}, dimensions={1}, use_global_device_ids=true | all-gather | bytes 12288 | tf_op jit(solution)/shard_map/all_gather | solution.py:156
  19.0 3.7 %compare_reduce_fusion = pred[4,768]{1,0:T(4,128)(4,1)S(1)} fusion(s32[2048]{0:T(1024)S(1)} %bitcast.103, s32[4,768]{1,0:T(4,128)S(1)} %multiply_add_fusion), kind=kLoop, calls=%fused_computation.28 | loop fusion | flops 12579840 | bytes 23552 | tf_op jit(solution)/shard_map/reduce_or | solution.py:163
  22.9 3.0 %fusion.23 = f32[2048]{0:T(1024)S(1)} fusion(f32[4,768]{1,0:T(4,128)S(1)} %fusion.24, s32[2048]{0:T(1024)S(1)} %bitcast.104, s32[4,768]{1,0:T(4,128)S(1)} %multiply_add_fusion), kind=kLoop, calls=%fused_computation.29 | loop fusion | flops 18872320 | bytes 40960 | tf_op jit(solution)/shard_map/reduce_sum | solution.py:167
  26.4 4.8 %dynamic-slice_bitcast_fusion = bf16[3,4,256,768]{3,2,1,0:T(8,128)(2,1)} fusion(bf16[3,4,2,256,768]{4,3,2,1,0:T(8,128)(2,1)} %bitcast.93, s32[]{:T(128)S(6)} %select_n.53), kind=kLoop, calls=%fused_computation.30 | loop fusion | bytes 9437188 | tf_op jit(solution)/shard_map/jit(dynamic_index_in_dim)/squeeze | solution.py:173
  31.2 0.6 reduce_max.9
  32.5 95.3 %conditional.1 = (f32[1024,512]{0,1:T(8,128)S(1)}) conditional(s32[]{:T(128)} %convert_element_type.35, (f32[]{:T(128)}, f32[2,1024]{1,0:T(2,128)S(1)}, s32[2,1024]{0,1:T(8,128)S(1)}, f32[768]{0:T(1024)S(1)}, pred[768]{0:T(1024)(128)(4,1)S(1)}, /*index=5*/bf16[3,4,256,768]{3,2,1,0:T(8,128)(2,1)}) %tuple.18, (f32[768]{0:T(1024)S(1)}, ...), branch_computations={%region_4.8_spmd, %region_8.9_spmd} | conditional | flops 4774863360 | bytes 91790768 | solution.py:212
  32.7 0.8 copy-done.1
  33.5 6.1 %convolution_convert_fusion.1 = bf16[432,3,4,256]{3,0,2,1:T(8,128)(2,1)} fusion(bf16[3,4,256,768]{3,2,1,0:T(8,128)(2,1)} %get-tuple-element.76, f32[768]{0:T(1024)S(1)} %get-tuple-element.74, pred[768]{0:T(1024)(128)(4,1)S(1)} %get-tuple-element.75), kind=kOutput, calls=%fused_computation.20 | convolution fusion | flops 2040422400 | bytes 7376640 | tf_op jit(solution)/shard_map/cond/branch_1_fun/dot_general | solution.py:181
  39.6 5.1 %reshape.71 = bf16[432,3,4,2,128]{4,3,0,2,1:T(2,128)(2,1)S(1)} reshape(bf16[432,3,4,256]{3,0,2,1:T(8,128)(2,1)} %convolution_convert_fusion.1) | data formatting | bytes 5308416 | tf_op jit(solution)/shard_map/cond/branch_1_fun/reshape | solution.py:184
  44.7 5.5 %copy.64 = bf16[432,3,4,2,128]{0,4,1,3,2:T(8,128)(2,1)} copy(bf16[432,3,4,2,128]{4,3,0,2,1:T(2,128)(2,1)S(1)} %reshape.71) | data formatting | bytes 5308416 | tf_op jit(solution)/shard_map/cond/branch_1_fun/reshape | solution.py:184
  50.3 3.5 %copy.65.chosen = bf16[4,2,432,384]{3,2,1,0:T(8,128)(2,1)S(1)} copy(bf16[4,2,432,384]{2,3,1,0:T(8,128)(2,1)} %bitcast.90) | data formatting | bytes 5308416 | tf_op jit(solution)/shard_map/cond/branch_1_fun/reshape | solution.py:188
  53.7 1.0 copy.70
  54.8 1.4 select_bitcast_fusion.slots
  56.2 68.3 %branch_1_fun.1 = f32[1024,512]{1,0:T(8,128)S(1)} custom-call(bf16[4,2,432,384]{3,2,1,0:T(8,128)(2,1)S(1)} %copy.65.chosen, s32[1024,2]{1,0:T(8,128)S(1)} %select_bitcast_fusion.slots), custom_call_target="tpu_custom_call" | custom-call | tf_op jit(solution)/shard_map/cond/branch_1_fun/pallas_call | solution.py:120
  124.5 1.4 copy-done
  125.9 1.9 copy.77
  128.0 1.3 collective-permute-start
  129.3 0.7 fusion.49
  131.5 8.0 %collective-permute-done = f32[10,512]{1,0:T(8,128)S(1)} collective-permute-done((f32[10,512]{1,0:T(8,128)S(1)}, f32[10,512]{1,0:T(8,128)S(1)}, u32[]{:S(2)}, u32[]{:S(2)}) %collective-permute-start) | collective-permute-done | bytes 20512 | tf_op jit(solution)/shard_map/ppermute | solution.py:215
  139.8 5.1 %fusion.25 = f32[1024,1024]{1,0:T(8,128)} fusion(f32[1024,512]{0,1:T(8,128)S(1)} %get-tuple-element.158, f32[512,512]{1,0:T(8,128)S(1)} %get-tuple-element.156, f32[512,512]{1,0:T(8,128)S(1)} %dynamic-slice_bitcast_fusion.2), kind=kOutput, calls=%fused_computation.33 | convolution fusion | flops 3221749760 | bytes 8388608 | tf_op jit(solution)/shard_map/dot_general | solution.py:15
  145.0 0.6 constant_dynamic-update-slice_fusion
  145.7 14.5 %all-gather.1 = f32[8,1,3200]{2,1,0:T(1,128)S(1)} all-gather(f32[1,1,3200]{2,1,0:T(1,128)S(1)} %reshape.78), channel_id=2, replica_groups=mesh['grp'=2,'atoms'=4,'feat'=2,'rep'=2] {'atoms','rep'}, dimensions={0}, use_global_device_ids=true | all-gather | bytes 115200 | tf_op jit(solution)/shard_map/all_gather | solution.py:233
  160.2 0.6 slice_reduce_fusion
  160.9 0.5 broadcast_divide_fusion
  161.7 0.6 add_rsqrt_fusion
  162.5 0.6 broadcast_divide_fusion.1
  163.1 0.6 add_rsqrt_fusion.1
  163.7 1.1 multiply_bitcast_fusion
  164.8 29.2 %reduce-scatter.2.cloned.1.call-done = f32[128,1024]{1,0:T(8,128)} async-done(((f32[1024,1024]{1,0:T(8,128)}), f32[128,1024]{1,0:T(8,128)}) %reduce-scatter.2.cloned.1.call-update) | async-done | bytes 524304 | tf_op jit(solution)/shard_map/reduce_scatter | solution.py:236
  194.0 1.7 convolution_add_fusion
  195.8 1.4 fusion.31
  (38 shorter events, 2.9 us)
Async XLA Ops:
  32.5 96.8 %copy-start.3 = (s32[1,2048]{1,0:T(1,128)S(1)}, s32[1,2048]{1,0:T(1,128)}, u32[]{:S(2)}) copy-start(s32[1,2048]{1,0:T(1,128)} %param.9) | copy-start | bytes 24580
  32.7 0.8 copy-start.1
  50.3 4.5 %copy-start.2 = (s32[2,1024]{0,1:T(8,128)S(1)}, s32[2,1024]{0,1:T(8,128)}, u32[]{:S(2)}) copy-start(s32[2,1024]{0,1:T(8,128)} %copy-done.1) | copy-start | bytes 24580 | tf_op jit(solution)/shard_map/cond
  124.5 1.4 copy-start
  127.8 66.3 %reduce-scatter.2.cloned.1.call-start = ((), (), s32[]{:S(2)}) async-start(), calls=%async_computation.3 | async-start | bytes 4718592 | tf_op jit(solution)/shard_map/reduce_scatter | solution.py:236
  128.0 11.5 %collective-permute-start = (f32[10,512]{1,0:T(8,128)S(1)}, f32[10,512]{1,0:T(8,128)S(1)}, u32[]{:S(2)}, u32[]{:S(2)}) collective-permute-start(f32[10,512]{1,0:T(8,128)S(1)} %slice.45), channel_id=1, source_target_pairs={{4,0},{8,4},{12,8},{5,1},{9,5},{13,9},{6,2},{10,6},{14,10},{7,3},{... | collective-permute-start | bytes 61448 | tf_op jit(solution)/shard_map/ppermute | solution.py:215
Sparse Core Ops, SparseCore 1:
  145.1 48.9 reduce-scatter.1

commit v3 on v2

--- a/solution.py
+++ b/solution.py
@@ -9,6 +9,7 @@
 from jax.sharding import PartitionSpec as P
 
 LAG = 10
+HALO = 16
 
 
 def matmul(left, right, dims, precision=None):
@@ -19,41 +20,89 @@
 MESH = pl.DeviceIdType.MESH
 
 
-def exchange_kernel(groups, feat_groups, room, lanes, chunks, tile, chosen, slots, out, sign, recv, *sems):
-    z_send, z_recv, z_own, x_send, x_recv = sems
+def exchange_kernel(
+    groups, feat_groups, room, lanes, chunks, tile, coords, picked, slots, out, halo, *scratch
+):
+    blocks, pick, chosen, sign, recv, edge, load, z_send, z_recv, z_own, x_send, x_recv, h_send, h_recv = scratch
     z, x = lax.axis_index("atoms"), lax.axis_index("feat")
     half = groups // 2
     z_steps = [half] + [o for o in range(groups - 1, 0, -1) if o != half] if groups > 1 else []
     x_steps = list(range(1, feat_groups))
     tiles = out.shape[0] // tile
+    frames_here = feat_groups * chunks * lanes
+    cols = halo.shape[1]
+    z_dests = [lax.rem(z + o, groups) for o in z_steps] + [z]
+    loads = []
+    for ch in range(chunks):
+        row = []
+        for i, dest in enumerate(z_dests):
+            start = pl.multiple_of(dest * frames_here + (x * chunks + ch) * lanes, 16)
+            row.append(
+                pltpu.make_async_copy(coords.at[:, pl.ds(start, lanes), :], blocks.at[ch, i], load.at[ch, i])
+            )
+            row[-1].start()
+        loads.append(row)
     barrier = pltpu.get_barrier_semaphore()
     for o in z_steps:
         pl.semaphore_signal(barrier, 1, device_id={"atoms": lax.rem(z + o, groups)}, device_id_type=MESH)
     for o in x_steps:
         pl.semaphore_signal(barrier, 1, device_id={"feat": lax.rem(x + o, feat_groups)}, device_id_type=MESH)
-    pl.semaphore_wait(barrier, len(z_steps) + len(x_steps))
+    z_up, z_down = lax.rem(z + 1, groups), lax.rem(z + groups - 1, groups)
+
+    @pl.when(x == 0)
+    def _():
+        for k in x_steps:
+            pl.semaphore_signal(barrier, 1, device_id={"atoms": z_down, "feat": k}, device_id_type=MESH)
+
+    @pl.when(x != 0)
+    def _():
+        pl.semaphore_signal(barrier, 1, device_id={"atoms": z_up, "feat": 0}, device_id_type=MESH)
+
+    width = picked.shape[1]
+    slot_no = lax.broadcasted_iota(jnp.int32, (room, width), 0)
+    pick[...] = jnp.where(slot_no == picked[...], 1.0, 0.0).astype(jnp.bfloat16)
+
+    @pl.when(x == 0)
+    def _():
+        pl.semaphore_wait(barrier, len(z_steps) + 2 * len(x_steps))
+
+    @pl.when(x != 0)
+    def _():
+        pl.semaphore_wait(barrier, len(z_steps) + len(x_steps) + 1)
+
+    def fill(ch, i):
+        loads[ch][i].wait()
+        for c in range(3):
+            got = lax.dot_general(
+                pick[...], blocks[ch, i, c], (((1,), (1,)), ((), ())), preferred_element_type=jnp.float32
+            )
+            chosen[ch, i, :, c * lanes : (c + 1) * lanes] = got.astype(jnp.bfloat16)
 
     here = pl.ds(pl.multiple_of(z * room, 16), room)
     z_copies = []
     for ch in range(chunks):
         row = []
         for i, o in enumerate(z_steps):
-            dest = lax.rem(z + o, groups)
+            fill(ch, i)
             row.append(
                 pltpu.make_async_remote_copy(
-                    src_ref=chosen.at[dest, ch],
+                    src_ref=chosen.at[ch, i],
                     dst_ref=recv.at[ch, here],
                     send_sem=z_send.at[ch, i],
                     recv_sem=z_recv.at[ch, i],
-                    device_id={"atoms": dest},
+                    device_id={"atoms": z_dests[i]},
                     device_id_type=MESH,
                 )
             )
             row[-1].start()
         z_copies.append(row)
-    own_copies = [pltpu.make_async_copy(chosen.at[z, ch], recv.at[ch, here], z_own.at[ch]) for ch in range(chunks)]
-    for copy in own_copies:
-        copy.start()
+    own_copies = []
+    for ch in range(chunks):
+        fill(ch, len(z_steps))
+        own_copies.append(
+            pltpu.make_async_copy(chosen.at[ch, len(z_steps)], recv.at[ch, here], z_own.at[ch])
+        )
+        own_copies[-1].start()
 
     place = lax.broadcasted_iota(jnp.int32, (128, groups * room), 1)
 
@@ -80,6 +129,16 @@
             device_id_type=MESH,
         )
 
+    def h_copy(k):
+        return pltpu.make_async_remote_copy(
+            src_ref=edge.at[:, k * cols : (k + 1) * cols],
+            dst_ref=halo,
+            send_sem=h_send.at[k],
+            recv_sem=h_recv.at[0],
+            device_id={"atoms": z_down, "feat": k},
+            device_id_type=MESH,
+        )
+
     for ch in range(chunks):
         own_copies[ch].wait()
         for copy in z_copies[ch]:
@@ -97,7 +156,22 @@
             return carry
 
         lax.fori_loop(0, tiles, features, 0)
-
+        if ch == 0:
+
+            @pl.when(x == 0)
+            def _():
+                for i in range(tiles):
+                    first = out[i * tile : (i + 1) * tile, :lanes]
+                    edge[:, i * tile : (i + 1) * tile] = first.T[:HALO]
+                for k in range(feat_groups):
+                    h_copy(k).start()
+
+    @pl.when(x == 0)
+    def _():
+        for k in range(feat_groups):
+            h_copy(k).wait_send()
+
+    h_copy(0).wait_recv()
     for ch in range(chunks):
         for copy in z_copies[ch]:
             copy.wait_send()
@@ -110,31 +184,41 @@
         lax.fori_loop(0, tiles, finish, 0)
 
 
-def exchange(chosen, slots, groups, feat_groups):
-    chunks, room, lanes = chosen.shape[1], chosen.shape[2], chosen.shape[3] // 3
-    feats = slots.shape[0]
+def exchange(coords, picked, slots, room, lanes, groups, feat_groups):
+    feats, width = slots.shape[0], picked.shape[1]
+    chunks = coords.shape[1] // (groups * feat_groups * lanes)
     tile = min(256, feats)
     vmem = pl.BlockSpec(memory_space=pltpu.VMEM)
     z_count, x_count = max(groups - 1, 1), max(feat_groups - 1, 1)
     dma = pltpu.SemaphoreType.DMA
     return pl.pallas_call(
         functools.partial(exchange_kernel, groups, feat_groups, room, lanes, chunks, tile),
-        out_shape=jax.ShapeDtypeStruct((feats, feat_groups * chunks * lanes), jnp.float32),
-        in_specs=[vmem, vmem],
-        out_specs=vmem,
+        out_shape=(
+            jax.ShapeDtypeStruct((feats, feat_groups * chunks * lanes), jnp.float32),
+            jax.ShapeDtypeStruct((HALO, feats // feat_groups), jnp.float32),
+        ),
+        in_specs=[pl.BlockSpec(memory_space=pl.ANY), vmem, vmem],
+        out_specs=(vmem, vmem),
         scratch_shapes=[
+            pltpu.VMEM((chunks, groups, 3, lanes, width), jnp.bfloat16),
+            pltpu.VMEM((room, width), jnp.bfloat16),
+            pltpu.VMEM((chunks, groups, room, 3 * lanes), jnp.bfloat16),
             pltpu.VMEM((feats, groups * room), jnp.bfloat16),
             pltpu.VMEM((chunks, groups * room, 3 * lanes), jnp.bfloat16),
+            pltpu.VMEM((HALO, feats), jnp.float32),
+            dma((chunks, groups)),
             dma((chunks, z_count)),
             dma((chunks, z_count)),
             dma((chunks,)),
             dma((chunks, feats // tile, x_count)),
             dma((chunks, feats // tile, x_count)),
+            dma((feat_groups,)),
+            dma((1,)),
         ],
         compiler_params=pltpu.CompilerParams(
             collective_id=0, has_side_effects=True, vmem_limit_bytes=48 * 1024 * 1024
         ),
-    )(chosen, slots)
+    )(coords, picked, slots)
 
 
 def slots_per_pass(width, refs, atoms):
@@ -169,31 +253,30 @@
     used_own = lax.dynamic_index_in_dim(used, z, 0, False)
     rank_own = lax.dynamic_index_in_dim(rank, z, 0, False)
 
-    grouped = jnp.transpose(atom_coords[0], (1, 0, 2)).reshape(3, groups, feat_groups, part, width)
-    blocks = lax.dynamic_index_in_dim(grouped, x, 2, False)
-
+    coords = jnp.transpose(atom_coords[0], (1, 0, 2))
     lanes = 128 if part % 128 == 0 else part
     chunks = part // lanes
 
-    def select(turn):
-        slot = jnp.arange(room, dtype=jnp.float32) + turn * jnp.float32(room)
-        pick = ((rank_own[None, :] == slot[:, None]) & used_own[None, :]).astype(jnp.bfloat16)
-        chosen = lax.dot_general(
-            pick, blocks, (((1,), (3,)), ((), ())), preferred_element_type=jnp.float32
-        ).astype(jnp.bfloat16)
-        chosen = jnp.transpose(chosen.reshape(room, 3, groups, chunks, lanes), (2, 3, 0, 1, 4))
+    def spots(turn):
         spot = ref_rank - turn * jnp.float32(room)
         inside = (spot >= 0) & (spot < room)
-        spot = jnp.where(inside, ref_shard * room + spot.astype(jnp.int32), -1)
-        return chosen.reshape(groups, chunks, room, 3 * lanes), spot.T
+        return jnp.where(inside, ref_shard * room + spot.astype(jnp.int32), -1).T
 
     def one_pass():
-        return exchange(*select(jnp.float32(0.0)), groups, feat_groups)
+        picked = jnp.where(used_own, rank_own.astype(jnp.int32), -1)[None]
+        return exchange(coords, picked, spots(jnp.float32(0.0)), room, lanes, groups, feat_groups)
 
     def more_passes():
         def step(carry):
             turn, delta = carry
-            chosen, spot = select(turn)
+            spot = spots(turn)
+            slot = jnp.arange(room, dtype=jnp.float32) + turn * jnp.float32(room)
+            pick = ((rank_own[None, :] == slot[:, None]) & used_own[None, :]).astype(jnp.bfloat16)
+            grouped = coords.reshape(3, groups, feat_groups, part, width)
+            blocks = lax.dynamic_index_in_dim(grouped, x, 2, False)
+            chosen = matmul(pick, blocks, ((1,), (3,))).astype(jnp.bfloat16)
+            chosen = jnp.transpose(chosen.reshape(room, 3, groups, chunks, lanes), (2, 3, 0, 1, 4))
+            chosen = chosen.reshape(groups, chunks, room, 3 * lanes)
             got = lax.all_to_all(chosen, "atoms", split_axis=0, concat_axis=0, tiled=True)
             got = jnp.transpose(got, (0, 2, 1, 3)).reshape(groups * room, chunks * 3 * lanes)
             place = jnp.arange(groups * room, dtype=jnp.int32)
@@ -207,13 +290,14 @@
         )
         delta = delta.reshape(feats, chunks, 3, lanes)
         computed = jnp.sqrt(jnp.sum(delta * delta, axis=2) + 0.01).reshape(feats, part)
-        return lax.all_gather(computed, "feat", axis=1, tiled=True)
-
-    every = lax.cond(most <= room, one_pass, more_passes).T
+        both = lax.all_gather(computed, "feat", axis=1, tiled=True)
+        first = lax.dynamic_slice_in_dim(both[:, :HALO], x * cols, cols, 0).T
+        return both, lax.ppermute(first, "atoms", [(i, (i - 1) % groups) for i in range(groups)])
+
+    every, incoming = lax.cond(most <= room, one_pass, more_passes)
+    every = every.T
     own = lax.dynamic_slice_in_dim(every, x * cols, cols, 1)
-    route = [(i, i - 1) for i in range(1, groups)]
-    incoming = lax.ppermute(own[:LAG], "atoms", route)
-    future = jnp.concatenate([own[LAG:], incoming], 0)
+    future = jnp.concatenate([own[LAG:], incoming[:LAG]], 0)
 
     ids = jnp.concatenate([traj_ids[0], jnp.full((LAG,), -1, jnp.int32)])
     ids_now = lax.dynamic_slice_in_dim(ids, z * frames_here, frames_here)

time: 205 us -> 179 us (0.87)
  local copies, waits for them, and re-layouts: 26.3 us -> 6.69 us
  waiting for transfers between devices: 37.2 us -> 30 us
  matrix products: 13.2 us -> 7.05 us
  blocking collectives: 24.4 us -> 30.4 us
    reshape x3 -> x0, local copies, waits for them, and re-layouts: 14.1 us -> none  [the longest x2 10.6 us: select(): chosen.reshape(room, 3, groups, chunks, lanes)]
    ppermute x1 -> x0, waiting for transfers between devices: 7.96 us -> none  [shards(): incoming = lax.ppermute(own[:LAG], 'atoms', route)]
    dot_general x1 -> x0, matrix products: 6.13 us -> none  [select(): lax.dot_general(pick, blocks, (((1,), (3,)), ((), ())), preferred_element...]
    all_gather x1, blocking collectives: 14.5 us -> 20.5 us  [shards(): stats = lax.all_gather(stats, ('atoms', 'rep'), axis=0, tiled=False)]
    squeeze x1 -> x0, local copies, waits for them, and re-layouts: 4.78 us -> none  [shards(): blocks = lax.dynamic_index_in_dim(grouped, x, 2, False)]
    cond x7 -> x2, local copies, waits for them, and re-layouts: 4.09 us -> 0.79 us
  transfers between devices with their start and end apart: 2 -> 1, of which waited for: 2 -> 1; matrix products, arithmetic and copies ran while one was open for 3% -> 3% of each run, Pallas kernels for 0% -> 0%
where the time goes in v3:
time: 179 us; the launch traced here: 178 us
  Pallas kernels  68.6 us (38%)
  blocking collectives  30.4 us (17%)
  waiting for transfers between devices  30 us (17%)
  other arithmetic  18.1 us (10%)
  between operations  17 us (9%)
  matrix products  7.05 us (4%)
  local copies, waits for them, and re-layouts  6.69 us (4%)
    pallas_call x1, Pallas kernels, exchange(): pl.pallas_call(functools.partial(exchange_kernel, groups, feat_groups, ro...  68.6 us
    reduce_scatter x1, waiting for transfers between devices, shards(): lax.psum_scatter(local, ('atoms', 'rep'), scatter_dimension=0, tiled=True)  30 us
    all_gather x1, blocking collectives, shards(): stats = lax.all_gather(stats, ('atoms', 'rep'), axis=0, tiled=False)  20.5 us
    all_gather x1, blocking collectives, shards(): pairs = lax.all_gather(atom_pairs, 'feat', axis=1, tiled=True)  9.94 us
    dot_general x3, matrix products, matmul(): lax.dot_general(left, right, (dims, ((), ())), precision=precision, prefe...  7.05 us
    reduce_or x1, other arithmetic, shards(): used = jnp.any(hit, axis=2)  3.68 us
  transfers between devices with their start and end apart: 1, of which 1 were waited for; matrix products, arithmetic and copies ran while one was open for 3% of the time, Pallas kernels for 0%

profile of v3, /device:TPU:0, one launch (start us, length us, event | category | flops | bytes accessed | tf_op | source)
XLA Modules:
  0.0 178.2 jit_solution(10439931698861005113)
XLA Ops:
  8.0 0.8 copy.60
  8.9 9.9 %all_gather.12 = s32[2,1024]{0,1:T(8,128)S(1)} all-gather(s32[2,512]{0,1:T(8,128)S(1)} %copy.60), channel_id=1, replica_groups=mesh['grp'=2,'atoms'=4,'feat'=2,'rep'=2] {'feat'}, dimensions={1}, use_global_device_ids=true | all-gather | bytes 12288 | tf_op jit(solution)/shard_map/all_gather | solution.py:240
  18.8 0.2 copy.61
  19.0 3.7 %compare_reduce_fusion = pred[4,768]{1,0:T(4,128)(4,1)S(1)} fusion(s32[2048]{0:T(1024)S(1)} %bitcast.96, s32[4,768]{1,0:T(4,128)S(1)} %multiply_add_fusion), kind=kLoop, calls=%fused_computation.27 | loop fusion | flops 12579840 | bytes 23552 | tf_op jit(solution)/shard_map/reduce_or | solution.py:247
  22.8 0.2 fusion.24
  23.0 0.4 add_select_fusion
  23.4 3.0 %fusion.23 = f32[2048]{0:T(1024)S(1)} fusion(f32[4,768]{1,0:T(4,128)S(1)} %fusion.24, s32[2048]{0:T(1024)S(1)} %bitcast.97, s32[4,768]{1,0:T(4,128)S(1)} %multiply_add_fusion), kind=kLoop, calls=%fused_computation.28 | loop fusion | flops 18872320 | bytes 40960 | tf_op jit(solution)/shard_map/reduce_sum | solution.py:251
  26.4 0.6 reduce_max.9
  27.7 0.7 fusion.49
  29.2 72.9 %conditional.1 = (f32[1024,512]{0,1:T(8,128)}, f32[10,512]{1,0:T(8,128)S(1)}) conditional(s32[]{:T(128)} %convert_element_type.42, (bf16[3,2048,768]{2,1,0:T(8,128)(2,1)}, s32[]{:T(128)}, f32[]{:T(128)}, f32[2,1024]{1,0:T(2,128)S(1)}, s32[2,1024]{0,1:T(8,128)S(1)}, /*index=5*/f32[768]{0:T(1024)S(1)}, pred[768]{0:T(1024)(128)(4,1)S(1)}) %tuple.80, ...), branch_computations={%region_4.8_spmd, %region_8.9_spmd} | conditional | flops 4774863360 | bytes 120430184 | solution.py:297
  29.4 0.8 copy-done.3
  30.2 0.2 copy.63
  30.4 1.2 select_bitcast_fusion.slots
  31.6 68.6 %branch_1_fun.1 = (f32[1024,512]{1,0:T(8,128)S(1)}, f32[16,512]{1,0:T(8,128)S(1)}) custom-call(bf16[3,2048,768]{2,1,0:T(8,128)(2,1)} %get-tuple-element.142.coords, s32[1,768]{1,0:T(1,128)S(1)} %broadcast_in_dim.30.picked, s32[1024,2]{1,0:T(8,128)S(1)} %select_bitcast_fusion.slots), custom_call_target="tpu_custom_call" | custom-call | tf_op jit(solution)/shard_map/cond/branch_1_fun/pallas_call | solution.py:194
  100.2 1.9 %copy.59 = f32[1024,512]{0,1:T(8,128)} copy(f32[1024,512]{1,0:T(8,128)S(1)} %get-tuple-element.239) | data formatting | bytes 4194304 | tf_op jit(solution)/shard_map
  102.1 1.9 %multiply_reduce_fusion.1 = f32[1024]{0:T(1024)S(1)} fusion(f32[1024,512]{0,1:T(8,128)} %get-tuple-element.154, f32[512]{0:T(512)S(1)} %get-tuple-element.284), kind=kLoop, calls=%fused_computation.37 | loop fusion | flops 1047552 | bytes 2103296 | tf_op jit(solution)/shard_map/reduce_sum | solution.py:309
  104.1 0.3 copy-done
  104.3 0.4 multiply_reduce_fusion
  104.7 1.4 dynamic-slice_bitcast_fusion.2
  106.4 0.2 multiply_reduce_fusion.2
  106.6 5.1 %fusion.25 = f32[1024,1024]{1,0:T(8,128)} fusion(f32[1024,512]{0,1:T(8,128)S(1)} %get-tuple-element.278, f32[512,512]{1,0:T(8,128)S(1)} %get-tuple-element.276, f32[512,512]{1,0:T(8,128)S(1)} %get-tuple-element.290), kind=kOutput, calls=%fused_computation.31 | convolution fusion | flops 3221749760 | bytes 8388608 | tf_op jit(solution)/shard_map/dot_general | solution.py:16
  111.8 0.7 constant_dynamic-update-slice_fusion
  112.5 20.5 %all-gather.1 = f32[8,1,3200]{2,1,0:T(1,128)S(1)} all-gather(f32[1,1,3200]{2,1,0:T(1,128)S(1)} %reshape.77), channel_id=2, replica_groups=mesh['grp'=2,'atoms'=4,'feat'=2,'rep'=2] {'atoms','rep'}, dimensions={0}, use_global_device_ids=true | all-gather | bytes 115200 | tf_op jit(solution)/shard_map/all_gather | solution.py:317
  133.0 0.6 slice_reduce_fusion
  133.8 0.5 broadcast_divide_fusion
  134.5 0.6 add_rsqrt_fusion
  135.3 0.5 broadcast_divide_fusion.1
  135.9 0.6 add_rsqrt_fusion.1
  136.5 1.1 multiply_bitcast_fusion
  137.6 30.0 %reduce-scatter.2.cloned.1.call-done = f32[128,1024]{1,0:T(8,128)} async-done(((f32[1024,1024]{1,0:T(8,128)}), f32[128,1024]{1,0:T(8,128)}) %reduce-scatter.2.cloned.1.call-update) | async-done | bytes 524304 | tf_op jit(solution)/shard_map/reduce_scatter | solution.py:320
  167.6 1.7 convolution_add_fusion
  169.3 1.4 fusion.31
  (30 shorter events, 1.1 us)
Async XLA Ops:
  8.0 19.7 %copy-start.4 = (s32[1,2048]{1,0:T(1,128)S(1)}, s32[1,2048]{1,0:T(1,128)}, u32[]{:S(2)}) copy-start(s32[1,2048]{1,0:T(1,128)} %param.9) | copy-start | bytes 24580
  29.4 0.8 copy-start.3
  102.1 65.5 %reduce-scatter.2.cloned.1.call-start = ((), (), s32[]{:S(2)}) async-start(), calls=%async_computation.3 | async-start | bytes 4718592 | tf_op jit(solution)/shard_map/reduce_scatter | solution.py:320
  102.1 2.2 %copy-start = (f32[1024,512]{0,1:T(8,128)S(1)}, f32[1024,512]{0,1:T(8,128)}, u32[]{:S(2)}) copy-start(f32[1024,512]{0,1:T(8,128)} %get-tuple-element.154) | copy-start | bytes 6291460
Sparse Core Ops, SparseCore 1:
  111.9 55.7 reduce-scatter.1

commit v4 on v3

--- a/solution.py
+++ b/solution.py
@@ -221,6 +221,159 @@
     )(coords, picked, slots)
 
 
+def reduce_kernel(groups, reps, local, stats, out, gathered, core, sums, left, right, *sems):
+    c_send, c_recv, s_own, s_send, s_recv, z_send, l_recv, r_recv = sems
+    z, r = lax.axis_index("atoms"), lax.axis_index("rep")
+    peers = [(a, b) for a in range(groups) for b in range(reps) if (a, b) != (0, 0)]
+    barrier = pltpu.get_barrier_semaphore()
+
+    def peer(a, b):
+        return {"atoms": lax.rem(z + a, groups), "rep": lax.rem(r + b, reps)}
+
+    for a, b in peers:
+        pl.semaphore_signal(barrier, 1, device_id=peer(a, b), device_id_type=MESH)
+    pl.semaphore_wait(barrier, len(peers))
+
+    order = []
+    for k in range((groups + 1) // 2):
+        order += [groups - 1 - k] + ([k] if k != groups - 1 - k else [])
+    core_copies = {}
+    for d in order:
+        for b in range(1, reps):
+            core_copies[d, b] = pltpu.make_async_remote_copy(
+                src_ref=local.at[d, lax.rem(r + b, reps)],
+                dst_ref=core.at[b - 1, d],
+                send_sem=c_send.at[b - 1, d],
+                recv_sem=c_recv.at[b - 1, d],
+                device_id={"rep": lax.rem(r + b, reps)},
+                device_id_type=MESH,
+            )
+            core_copies[d, b].start()
+    me = z * reps + r
+    own = pltpu.make_async_copy(stats, gathered.at[me], s_own.at[0])
+    own.start()
+    stat_copies = []
+    for k, (a, b) in enumerate(peers):
+        stat_copies.append(
+            pltpu.make_async_remote_copy(
+                src_ref=stats,
+                dst_ref=gathered.at[me],
+                send_sem=s_send.at[k],
+                recv_sem=s_recv.at[k],
+                device_id=peer(a, b),
+                device_id_type=MESH,
+            )
+        )
+        stat_copies[-1].start()
+
+
+    def hop(d, step):
+        return pltpu.make_async_remote_copy(
+            src_ref=sums.at[d],
+            dst_ref=(left if step > 0 else right).at[d],
+            send_sem=z_send.at[d],
+            recv_sem=(l_recv if step > 0 else r_recv).at[d],
+            device_id={"atoms": lax.rem(z + step + groups, groups)},
+            device_id_type=MESH,
+        )
+
+    for d in order:
+        total = local[d, r]
+        for b in range(1, reps):
+            core_copies[d, b].wait_recv()
+            total = total + core[b - 1, d]
+        sums[d] = total
+
+        if d > 0:
+
+            @pl.when(z == 0)
+            def _(d=d):
+                hop(d, 1).start()
+
+        if d < groups - 1:
+
+            @pl.when(z == groups - 1)
+            def _(d=d):
+                hop(d, -1).start()
+
+    for k in range(groups):
+        up, down = groups - 1 - k, k
+
+        @pl.when((z > 0) & (z < up))
+        def _(d=up):
+            hop(d, 1).wait_recv()
+            sums[d] = sums[d] + left[d]
+            hop(d, 1).start()
+
+        @pl.when((z < groups - 1) & (z > down))
+        def _(d=down):
+            hop(d, -1).wait_recv()
+            sums[d] = sums[d] + right[d]
+            hop(d, -1).start()
+
+    for d in range(groups):
+
+        @pl.when(z == d)
+        def _(d=d):
+            total = sums[d]
+            if d > 0:
+                hop(d, 1).wait_recv()
+                total = total + left[d]
+            if d < groups - 1:
+                hop(d, -1).wait_recv()
+                total = total + right[d]
+            out[...] = total
+
+        @pl.when(z < d)
+        def _(d=d):
+            hop(d, 1).wait_send()
+
+        @pl.when(z > d)
+        def _(d=d):
+            hop(d, -1).wait_send()
+
+    for copy in core_copies.values():
+        copy.wait_send()
+    own.wait()
+    for copy in stat_copies:
+        copy.wait()
+
+
+def reduce_blocks(local, stats, groups, reps):
+    rows, width = local.shape[0] // (groups * reps), local.shape[1]
+    vmem = pl.BlockSpec(memory_space=pltpu.VMEM)
+    dma = pltpu.SemaphoreType.DMA
+    block = pltpu.VMEM((groups, rows, width), jnp.float32)
+    others = max(groups * reps - 1, 1)
+    others_core = max(reps - 1, 1)
+    return pl.pallas_call(
+        functools.partial(reduce_kernel, groups, reps),
+        out_shape=(
+            jax.ShapeDtypeStruct((rows, width), jnp.float32),
+            jax.ShapeDtypeStruct((groups * reps,) + stats.shape, jnp.float32),
+        ),
+        in_specs=[vmem, vmem],
+        out_specs=(vmem, vmem),
+        scratch_shapes=[
+            pltpu.VMEM((others_core, groups, rows, width), jnp.float32),
+            block,
+            block,
+            block,
+            dma((others_core, groups)),
+            dma((others_core, groups)),
+            dma((1,)),
+            dma((others,)),
+            dma((others,)),
+            dma((groups,)),
+            dma((groups,)),
+            dma((groups,)),
+        ],
+        compiler_params=pltpu.CompilerParams(
+            collective_id=1, has_side_effects=True, vmem_limit_bytes=48 * 1024 * 1024
+        ),
+    )(local.reshape(groups, reps, rows, width), stats)
+
+
 def slots_per_pass(width, refs, atoms):
     share = width * (1.0 - math.exp(-refs / atoms)) + 2.05 * math.sqrt(width)
     return min(-(-width // 16) * 16, -(-int(share) // 16) * 16)
@@ -290,7 +443,10 @@
         )
         delta = delta.reshape(feats, chunks, 3, lanes)
         computed = jnp.sqrt(jnp.sum(delta * delta, axis=2) + 0.01).reshape(feats, part)
-        both = lax.all_gather(computed, "feat", axis=1, tiled=True)
+        both = jnp.zeros((feats, frames_here), jnp.float32)
+        for o in range(feat_groups):
+            turned = lax.ppermute(computed, "feat", [(i, (i + o) % feat_groups) for i in range(feat_groups)])
+            both = lax.dynamic_update_slice_in_dim(both, turned, ((x - o) % feat_groups) * part, 1)
         first = lax.dynamic_slice_in_dim(both[:, :HALO], x * cols, cols, 0).T
         return both, lax.ppermute(first, "atoms", [(i, (i - 1) % groups) for i in range(groups)])
 
@@ -314,12 +470,13 @@
     stats = jnp.concatenate(
         [now_b, next_b, jnp.sum(now_c * now_c, 0), jnp.sum(next_c * next_c, 0), jnp.full((128,), count_b)]
     )
-    stats = lax.all_gather(stats, ("atoms", "rep"), axis=0, tiled=False)
-
+    reps = lax.axis_size("rep")
+    stats = jnp.pad(stats, (0, -stats.shape[0] % 1024)).reshape(-1, 128)
     local = matmul(now_c, jnp.concatenate([own_c, next_c], 1), ((0,), (0,)), lax.Precision.HIGH)
-    mine = lax.psum_scatter(local, ("atoms", "rep"), scatter_dimension=0, tiled=True)
-
-    counts = stats[:, -1:]
+    mine, stats = reduce_blocks(local, stats, groups, reps)
+    stats = stats.reshape(groups * reps, -1)
+
+    counts = stats[:, 2 * feats + 2 * cols :][:, :1]
     now_all = stats[:, :feats]
     next_all = stats[:, feats : feats + cols]
     sq_now = stats[:, feats + cols : 2 * feats + cols]

time: 179 us -> 172 us (0.961)
  Pallas kernels: 68.6 us -> 129 us
  waiting for transfers between devices: 30 us -> 0 us
  blocking collectives: 30.4 us -> 9.94 us
  between operations: 17 us -> 2.19 us
  matrix products: 7.05 us -> 4.46 us
    pallas_call x0 -> x1, Pallas kernels: none -> 60.9 us  [reduce_blocks(): pl.pallas_call(functools.partial(reduce_kernel, groups, reps), out_shape=...]
    reduce_scatter x1 -> x0, waiting for transfers between devices: 30 us -> none  [shards(): lax.psum_scatter(local, ('atoms', 'rep'), scatter_dimension=0, tiled=True)]
    all_gather x1 -> x0, blocking collectives: 20.5 us -> none  [shards(): stats = lax.all_gather(stats, ('atoms', 'rep'), axis=0, tiled=False)]
    dot_general x3, matrix products: 7.05 us -> 4.46 us  [matmul(): lax.dot_general(left, right, (dims, ((), ())), precision=precision, prefe...]
  transfers between devices with their start and end apart: 1 -> 0, of which waited for: 1 -> 0; matrix products, arithmetic and copies ran while one was open for 3% -> 0% of each run, Pallas kernels for 0% -> 0%
where the time goes in v4:
time: 172 us; the launch traced here: 171 us
  Pallas kernels  129 us (75%)
  other arithmetic  19.2 us (11%)
  blocking collectives  9.94 us (6%)
  local copies, waits for them, and re-layouts  5.82 us (3%)
  matrix products  4.46 us (3%)
  between operations  2.19 us (1%)
    pallas_call x1, Pallas kernels, exchange(): pl.pallas_call(functools.partial(exchange_kernel, groups, feat_groups, ro...  68.6 us
    pallas_call x1, Pallas kernels, reduce_blocks(): pl.pallas_call(functools.partial(reduce_kernel, groups, reps), out_shape=...  60.9 us
    all_gather x1, blocking collectives, shards(): pairs = lax.all_gather(atom_pairs, 'feat', axis=1, tiled=True)  9.94 us
    dot_general x3, matrix products, matmul(): lax.dot_general(left, right, (dims, ((), ())), precision=precision, prefe...  4.46 us
    reduce_or x1, other arithmetic, shards(): used = jnp.any(hit, axis=2)  3.68 us

profile of v4, /device:TPU:0, one launch (start us, length us, event | category | flops | bytes accessed | tf_op | source)
XLA Modules:
  0.0 171.4 jit_solution(3960003075280894566)
XLA Ops:
  0.6 0.8 copy.49
  1.5 9.9 %all_gather.3 = s32[2,1024]{0,1:T(8,128)S(1)} all-gather(s32[2,512]{0,1:T(8,128)S(1)} %copy.49), channel_id=1, replica_groups=mesh['grp'=2,'atoms'=4,'feat'=2,'rep'=2] {'feat'}, dimensions={1}, use_global_device_ids=true | all-gather | bytes 12288 | tf_op jit(solution)/shard_map/all_gather | solution.py:393
  11.4 0.2 copy.50
  11.6 3.7 %compare_reduce_fusion = pred[4,768]{1,0:T(4,128)(4,1)S(1)} fusion(s32[2048]{0:T(1024)S(1)} %bitcast.109, s32[4,768]{1,0:T(4,128)S(1)} %multiply_add_fusion), kind=kLoop, calls=%fused_computation.29 | loop fusion | flops 12579840 | bytes 23552 | tf_op jit(solution)/shard_map/reduce_or | solution.py:400
  15.3 0.2 fusion.24
  15.6 3.0 %fusion.23 = f32[2048]{0:T(1024)S(1)} fusion(f32[4,768]{1,0:T(4,128)S(1)} %fusion.24, s32[2048]{0:T(1024)S(1)} %bitcast.110, s32[4,768]{1,0:T(4,128)S(1)} %multiply_add_fusion), kind=kLoop, calls=%fused_computation.30 | loop fusion | flops 18872320 | bytes 40960 | tf_op jit(solution)/shard_map/reduce_sum | solution.py:404
  18.6 0.1 convert_reduce_fusion
  18.7 0.6 reduce_max.9
  19.3 0.3 add_select_fusion
  20.3 71.1 %conditional.1 = (f32[1024,512]{0,1:T(8,128)}, f32[10,512]{1,0:T(8,128)S(1)}) conditional(s32[]{:T(128)} %convert_element_type.44, (bf16[3,2048,768]{2,1,0:T(8,128)(2,1)}, s32[]{:T(128)}, f32[]{:T(128)}, f32[2,1024]{1,0:T(2,128)S(1)}, s32[2,1024]{0,1:T(8,128)S(1)}, /*index=5*/f32[768]{0:T(1024)S(1)}, pred[768]{0:T(1024)(128)(4,1)S(1)}) %tuple.72, ...), branch_computations={%region_4.8_spmd, %region_8.9_spmd} | conditional | flops 4774863360 | bytes 125673448 | solution.py:453
  20.6 0.2 copy.52
  20.8 0.1 select_bitcast_fusion.slots
  21.0 68.6 %branch_1_fun.1 = (f32[1024,512]{1,0:T(8,128)S(1)}, f32[16,512]{1,0:T(8,128)S(1)}) custom-call(bf16[3,2048,768]{2,1,0:T(8,128)(2,1)} %get-tuple-element.142.coords, s32[1,768]{1,0:T(1,128)S(1)} %broadcast_in_dim.30.picked, s32[1024,2]{1,0:T(8,128)S(1)} %select_bitcast_fusion.slots), custom_call_target="tpu_custom_call" | custom-call | tf_op jit(solution)/shard_map/cond/branch_1_fun/pallas_call | solution.py:194
  89.5 1.9 %copy.48 = f32[1024,512]{0,1:T(8,128)} copy(f32[1024,512]{1,0:T(8,128)S(1)} %get-tuple-element.221) | data formatting | bytes 4194304 | tf_op jit(solution)/shard_map
  91.4 0.7 fusion.49
  92.1 1.8 %multiply_reduce_fusion.1 = f32[1024]{0:T(1024)S(1)} fusion(f32[1024,512]{0,1:T(8,128)} %get-tuple-element.156, f32[512]{0:T(512)S(1)} %get-tuple-element.264), kind=kLoop, calls=%fused_computation.39 | loop fusion | flops 1047552 | bytes 2103296 | tf_op jit(solution)/shard_map/reduce_sum | solution.py:465
  94.6 2.0 %multiply_reduce_fusion = (f32[1024]{0:T(1024)S(1)}, f32[1024,512]{0,1:T(8,128)S(1)}) fusion(f32[1024,512]{0,1:T(8,128)} %get-tuple-element.156, f32[1024]{0:T(1024)S(1)} %get-tuple-element.262, f32[512]{0:T(512)S(1)} %get-tuple-element.264), kind=kLoop, calls=%fused_computation.37 | loop fusion | flops 2096128 | bytes 4204544 | tf_op jit(solution)/shard_map/reduce_sum | solution.py:471
  96.6 1.4 dynamic-slice_bitcast_fusion.2
  98.0 0.1 slice.58
  98.2 0.2 multiply_reduce_fusion.3
  98.3 0.2 multiply_reduce_fusion.2
  98.6 0.6 constant_dynamic-update-slice_fusion.2
  99.2 3.5 %fusion.25 = f32[1024,1024]{1,0:T(8,128)S(1)} fusion(f32[1024,512]{0,1:T(8,128)S(1)} %get-tuple-element.258, f32[512,512]{1,0:T(8,128)S(1)} %get-tuple-element.256, f32[512,512]{1,0:T(8,128)S(1)} %get-tuple-element.272), kind=kOutput, calls=%fused_computation.33 | convolution fusion | flops 3221749760 | bytes 8388608 | tf_op jit(solution)/shard_map/dot_general | solution.py:16
  102.8 60.9 %shard_map.58 = (f32[128,1024]{1,0:T(8,128)S(1)}, f32[8,32,128]{2,1,0:T(8,128)S(1)}) custom-call(f32[4,2,128,1024]{3,2,1,0:T(8,128)S(1)} %bitcast.81, f32[32,128]{1,0:T(8,128)S(1)} %pad_bitcast_fusion.stats), custom_call_target="tpu_custom_call" | custom-call | tf_op jit(solution)/shard_map/pallas_call | solution.py:349
  163.8 0.7 slice_reduce_fusion
  164.6 0.7 broadcast_divide_fusion
  165.4 0.7 add_rsqrt_fusion
  166.3 1.1 multiply_bitcast_fusion
  167.6 0.7 broadcast_divide_fusion.1
  168.3 0.7 add_rsqrt_fusion.1
  169.1 0.7 convolution_add_fusion
  169.8 1.6 fusion.31
  (24 shorter events, 0.9 us)
Async XLA Ops:
  20.3 71.1 %copy-start.2 = (s32[1,2048]{1,0:T(1,128)S(1)}, s32[1,2048]{1,0:T(1,128)}, u32[]{:S(2)}) copy-start(s32[1,2048]{1,0:T(1,128)} %param.9) | copy-start | bytes 24580

commit v5 on v4

--- a/solution.py
+++ b/solution.py
@@ -277,6 +277,7 @@
             device_id_type=MESH,
         )
 
+    ready, sent = set(), 0
     for d in order:
         total = local[d, r]
         for b in range(1, reps):
@@ -290,11 +291,14 @@
             def _(d=d):
                 hop(d, 1).start()
 
-        if d < groups - 1:
+        ready.add(d)
+        while sent < groups - 1 and sent in ready:
 
             @pl.when(z == groups - 1)
-            def _(d=d):
+            def _(d=sent):
                 hop(d, -1).start()
+
+            sent += 1
 
     for k in range(groups):
         up, down = groups - 1 - k, k

time: 172 us -> 172 us (level)
  no operation moved by 1% of the time
where the time goes in v5:
time: 172 us; the launch traced here: 171 us
  Pallas kernels  129 us (75%)
  other arithmetic  19.2 us (11%)
  blocking collectives  9.94 us (6%)
  local copies, waits for them, and re-layouts  5.82 us (3%)
  matrix products  4.46 us (3%)
  between operations  2.19 us (1%)
    pallas_call x1, Pallas kernels, exchange(): pl.pallas_call(functools.partial(exchange_kernel, groups, feat_groups, ro...  68.6 us
    pallas_call x1, Pallas kernels, reduce_blocks(): pl.pallas_call(functools.partial(reduce_kernel, groups, reps), out_shape=...  60.9 us
    all_gather x1, blocking collectives, shards(): pairs = lax.all_gather(atom_pairs, 'feat', axis=1, tiled=True)  9.94 us
    dot_general x3, matrix products, matmul(): lax.dot_general(left, right, (dims, ((), ())), precision=precision, prefe...  4.46 us
    reduce_or x1, other arithmetic, shards(): used = jnp.any(hit, axis=2)  3.68 us

profile of v5, /device:TPU:0, one launch (start us, length us, event | category | flops | bytes accessed | tf_op | source)
XLA Modules:
  0.0 171.4 jit_solution(6958424606394571417)
XLA Ops:
  0.6 0.8 copy.49
  1.5 9.9 %all_gather.3 = s32[2,1024]{0,1:T(8,128)S(1)} all-gather(s32[2,512]{0,1:T(8,128)S(1)} %copy.49), channel_id=1, replica_groups=mesh['grp'=2,'atoms'=4,'feat'=2,'rep'=2] {'feat'}, dimensions={1}, use_global_device_ids=true | all-gather | bytes 12288 | tf_op jit(solution)/shard_map/all_gather | solution.py:397
  11.4 0.2 copy.50
  11.6 3.7 %compare_reduce_fusion = pred[4,768]{1,0:T(4,128)(4,1)S(1)} fusion(s32[2048]{0:T(1024)S(1)} %bitcast.109, s32[4,768]{1,0:T(4,128)S(1)} %multiply_add_fusion), kind=kLoop, calls=%fused_computation.29 | loop fusion | flops 12579840 | bytes 23552 | tf_op jit(solution)/shard_map/reduce_or | solution.py:404
  15.3 0.2 fusion.24
  15.6 3.0 %fusion.23 = f32[2048]{0:T(1024)S(1)} fusion(f32[4,768]{1,0:T(4,128)S(1)} %fusion.24, s32[2048]{0:T(1024)S(1)} %bitcast.110, s32[4,768]{1,0:T(4,128)S(1)} %multiply_add_fusion), kind=kLoop, calls=%fused_computation.30 | loop fusion | flops 18872320 | bytes 40960 | tf_op jit(solution)/shard_map/reduce_sum | solution.py:408
  18.6 0.1 convert_reduce_fusion
  18.7 0.6 reduce_max.9
  19.3 0.3 add_select_fusion
  20.3 71.1 %conditional.1 = (f32[1024,512]{0,1:T(8,128)}, f32[10,512]{1,0:T(8,128)S(1)}) conditional(s32[]{:T(128)} %convert_element_type.44, (bf16[3,2048,768]{2,1,0:T(8,128)(2,1)}, s32[]{:T(128)}, f32[]{:T(128)}, f32[2,1024]{1,0:T(2,128)S(1)}, s32[2,1024]{0,1:T(8,128)S(1)}, /*index=5*/f32[768]{0:T(1024)S(1)}, pred[768]{0:T(1024)(128)(4,1)S(1)}) %tuple.72, ...), branch_computations={%region_4.8_spmd, %region_8.9_spmd} | conditional | flops 4774863360 | bytes 125673448 | solution.py:457
  20.6 0.2 copy.52
  20.8 0.1 select_bitcast_fusion.slots
  21.0 68.6 %branch_1_fun.1 = (f32[1024,512]{1,0:T(8,128)S(1)}, f32[16,512]{1,0:T(8,128)S(1)}) custom-call(bf16[3,2048,768]{2,1,0:T(8,128)(2,1)} %get-tuple-element.142.coords, s32[1,768]{1,0:T(1,128)S(1)} %broadcast_in_dim.30.picked, s32[1024,2]{1,0:T(8,128)S(1)} %select_bitcast_fusion.slots), custom_call_target="tpu_custom_call" | custom-call | tf_op jit(solution)/shard_map/cond/branch_1_fun/pallas_call | solution.py:194
  89.5 1.9 %copy.48 = f32[1024,512]{0,1:T(8,128)} copy(f32[1024,512]{1,0:T(8,128)S(1)} %get-tuple-element.221) | data formatting | bytes 4194304 | tf_op jit(solution)/shard_map
  91.4 0.7 fusion.49
  92.1 1.8 %multiply_reduce_fusion.1 = f32[1024]{0:T(1024)S(1)} fusion(f32[1024,512]{0,1:T(8,128)} %get-tuple-element.156, f32[512]{0:T(512)S(1)} %get-tuple-element.264), kind=kLoop, calls=%fused_computation.39 | loop fusion | flops 1047552 | bytes 2103296 | tf_op jit(solution)/shard_map/reduce_sum | solution.py:469
  94.6 2.0 %multiply_reduce_fusion = (f32[1024]{0:T(1024)S(1)}, f32[1024,512]{0,1:T(8,128)S(1)}) fusion(f32[1024,512]{0,1:T(8,128)} %get-tuple-element.156, f32[1024]{0:T(1024)S(1)} %get-tuple-element.262, f32[512]{0:T(512)S(1)} %get-tuple-element.264), kind=kLoop, calls=%fused_computation.37 | loop fusion | flops 2096128 | bytes 4204544 | tf_op jit(solution)/shard_map/reduce_sum | solution.py:475
  96.6 1.4 dynamic-slice_bitcast_fusion.2
  98.0 0.1 slice.58
  98.2 0.2 multiply_reduce_fusion.3
  98.3 0.2 multiply_reduce_fusion.2
  98.6 0.6 constant_dynamic-update-slice_fusion.2
  99.2 3.5 %fusion.25 = f32[1024,1024]{1,0:T(8,128)S(1)} fusion(f32[1024,512]{0,1:T(8,128)S(1)} %get-tuple-element.258, f32[512,512]{1,0:T(8,128)S(1)} %get-tuple-element.256, f32[512,512]{1,0:T(8,128)S(1)} %get-tuple-element.272), kind=kOutput, calls=%fused_computation.33 | convolution fusion | flops 3221749760 | bytes 8388608 | tf_op jit(solution)/shard_map/dot_general | solution.py:16
  102.8 60.9 %shard_map.58 = (f32[128,1024]{1,0:T(8,128)S(1)}, f32[8,32,128]{2,1,0:T(8,128)S(1)}) custom-call(f32[4,2,128,1024]{3,2,1,0:T(8,128)S(1)} %bitcast.81, f32[32,128]{1,0:T(8,128)S(1)} %pad_bitcast_fusion.stats), custom_call_target="tpu_custom_call" | custom-call | tf_op jit(solution)/shard_map/pallas_call | solution.py:353
  163.8 0.7 slice_reduce_fusion
  164.6 0.7 broadcast_divide_fusion
  165.4 0.7 add_rsqrt_fusion
  166.3 1.1 multiply_bitcast_fusion
  167.6 0.7 broadcast_divide_fusion.1
  168.3 0.7 add_rsqrt_fusion.1
  169.1 0.7 convolution_add_fusion
  169.8 1.6 fusion.31
  (24 shorter events, 0.9 us)
Async XLA Ops:
  20.3 71.1 %copy-start.2 = (s32[1,2048]{1,0:T(1,128)S(1)}, s32[1,2048]{1,0:T(1,128)}, u32[]{:S(2)}) copy-start(s32[1,2048]{1,0:T(1,128)} %param.9) | copy-start | bytes 24580
